TPU v7x, 128 devices: a whole 4x4x4 slice. The times are simulated.
128 devices in a mesh: ctx: 32 (over y, z, core), exp: 4 (over x).
Axes of the slice: x: 4, y: 4, z: 4, core: 2. Of those that a mesh axis runs over, the one named last changes fastest.
Arguments:
- queries: bfloat16 [16384, 4096], P('ctx', 'exp'), may hold values from -6 to 6
- key_vectors: bfloat16 [16384, 4096], P('ctx', 'exp'), may hold values from -6 to 6
- value_vectors: bfloat16 [16384, 4096], P('ctx', 'exp'), may hold values from -6 to 6
- spikes: int32 [16384, 32], P('ctx', 'exp'), may hold values 0 or 1
- routes: int32 [16384, 2], P(('ctx', 'exp')), may hold values from 0 to 63, all different within a row; in each aligned block of 128 rows (0 to 127, 128 to 255, ...) at most 6 rows name the same one
- route_probs: bfloat16 [16384, 2], P(('ctx', 'exp')), may hold values from 0.099609375 to 1
- gate_weight: bfloat16 [128, 4096, 384], P(('ctx', 'exp')), may hold values from -0.09375 to 0.09375
- up_weight: bfloat16 [128, 4096, 384], P(('ctx', 'exp')), may hold values from -0.09375 to 0.09375
- down_weight: bfloat16 [128, 384, 4096], P(('ctx', 'exp')), may hold values from -0.21875 to 0.21875
- out_grad: bfloat16 [16384, 4096], P(('ctx', 'exp')), may hold values from -6 to 6
Outputs:
- grad_queries: bfloat16 [16384, 4096], P('ctx', 'exp')
- grad_keys: bfloat16 [16384, 4096], P('ctx', 'exp')
- grad_values: bfloat16 [16384, 4096], P('ctx', 'exp')
- grad_gate: bfloat16 [128, 4096, 384], P(('ctx', 'exp'))
- grad_up: bfloat16 [128, 4096, 384], P(('ctx', 'exp'))
- grad_down: bfloat16 [128, 384, 4096], P(('ctx', 'exp'))
Inputs may be any that keep to these rules, and one draw needn't show every extreme that they name: The 2 experts of a token differ. Among the routes of one route block of 128 positions no expert is named more than 6 times, and in some blocks one expert is named exactly 6 times.
All inputs are finite; a program needn't handle non-finite values. No bound on the sum of `spikes` on one device may be relied on, other than what follows from the above.
Results may differ from a plain program's by a relative error of at most 0.015.
Values may be sent and summed in bfloat16 or wider, within the bound.
No kernel may reach another device: no remote copies, remote signals or barrier semaphores. Data moves between devices by JAX's collectives and lax.ppermute only.
A program may use at most 192 MiB of HBM per device.

v0:
```python
import math

import jax
import jax.numpy as jnp
from jax import lax
from jax.sharding import PartitionSpec as P


def prefix(part, axis, combine, identity):
    place = lax.axis_index(axis)
    gathered = lax.all_gather(part, axis)
    state = jnp.zeros_like(part) + jnp.asarray(identity, part.dtype)

    def prefix_one(turn, state):
        return combine(state, lax.dynamic_index_in_dim(gathered, turn, 0, False))

    return lax.fori_loop(0, place, prefix_one, state)


def carried_in(x, axis, join, neutral):
    count = lax.axis_size(axis)
    place = lax.axis_index(axis)
    ahead = count - 1 - place
    gathered = lax.all_gather(x.astype(jnp.bfloat16), axis)
    state = jnp.zeros_like(x) + jnp.asarray(neutral, x.dtype)

    def carried_one(turn, state):
        source = count - 1 - turn
        return join(state, lax.dynamic_index_in_dim(gathered, source, 0, False).astype(x.dtype))

    return lax.fori_loop(0, ahead, carried_one, state)


def add_states(first_part, second_part):
    return first_part + second_part


def on_device(
    queries,
    key_vectors,
    value_vectors,
    spikes,
    routes,
    route_probs,
    gate_weight,
    up_weight,
    down_weight,
    out_grad,
):
    block_len = queries.shape[0]
    local_width = queries.shape[1]
    head_count = spikes.shape[1]
    head_size = local_width // head_count
    tok_rows = out_grad.shape[0]
    model_width = out_grad.shape[1]
    top_count = routes.shape[1]
    ctx_count = lax.axis_size("ctx")
    exp_count = lax.axis_size("exp")
    device_count = ctx_count * exp_count
    expert_count = device_count // 2
    capacity = 2 * max(1, 3 * tok_rows * top_count // (4 * expert_count))
    scaling = 1.0 / math.sqrt(head_size * block_len * ctx_count)
    highest = lax.Precision.HIGHEST
    query = queries.reshape(block_len, head_count, head_size)
    key_heads = key_vectors.reshape(block_len, head_count, head_size)
    value_heads = value_vectors.reshape(block_len, head_count, head_size)
    spike_gate = spikes.astype(jnp.bfloat16)[:, :, None]
    masked_keys = key_heads * spike_gate
    positions = jnp.arange(block_len)
    causal = (positions[:, None] >= positions[None, :])[None]
    block_state = jnp.einsum(
        "shi,shj->hij", masked_keys, value_heads, preferred_element_type=jnp.float32
    )
    states_in = prefix(block_state, "ctx", add_states, jnp.zeros_like(block_state))
    scores = jnp.einsum("thd,shd->hts", query, masked_keys, preferred_element_type=jnp.float32)
    scores = jnp.where(causal, scores, 0.0).astype(jnp.bfloat16)
    intra = jnp.einsum("hts,shd->thd", scores, value_heads, preferred_element_type=jnp.float32)
    inter = jnp.einsum("thi,hij->thj", query.astype(jnp.float32), states_in, precision=highest)
    attended = (scaling * (intra + inter)).astype(jnp.bfloat16).reshape(block_len, local_width)
    token_rows = lax.all_to_all(attended, "exp", split_axis=0, concat_axis=1, tiled=True)
    flat_route = routes.reshape(-1)
    expert_ids = jnp.arange(expert_count, dtype=jnp.int32)
    onehot = (flat_route[:, None] == expert_ids[None, :]).astype(jnp.int32)
    earlier = jnp.cumsum(onehot, axis=0) - onehot
    slot_index = jnp.sum(earlier * onehot, axis=1)
    target = flat_route * capacity + slot_index
    slot_ids = jnp.arange(expert_count * capacity, dtype=jnp.int32)
    hit_table = (slot_ids[:, None] == target[None, :]).reshape(
        expert_count * capacity, tok_rows, top_count
    )
    dispatch = jnp.sum(hit_table.astype(jnp.float32), axis=2).astype(jnp.bfloat16)
    weighted = jnp.sum(
        jnp.where(hit_table, route_probs.astype(jnp.float32)[None], 0.0), axis=2
    ).astype(jnp.bfloat16)
    send_rows = jnp.dot(dispatch, token_rows, preferred_element_type=jnp.float32).astype(
        jnp.bfloat16
    )
    send_grads = jnp.dot(weighted, out_grad, preferred_element_type=jnp.float32).astype(
        jnp.bfloat16
    )

    def duplicate(slot_rows):
        spread = jnp.broadcast_to(
            slot_rows.reshape(expert_count, 1, capacity, model_width),
            (expert_count, 2, capacity, model_width),
        )
        return spread.reshape(device_count, capacity, model_width)

    row_copies = duplicate(send_rows)
    grad_copies = duplicate(send_grads)
    got_rows, got_grads = (
        lax.all_to_all(row_copies, ("ctx", "exp"), split_axis=0, concat_axis=0, tiled=True),
        lax.all_to_all(grad_copies, ("ctx", "exp"), split_axis=0, concat_axis=0, tiled=True),
    )
    expert_rows = got_rows.reshape(-1, model_width)
    grad_rows = got_grads.reshape(-1, model_width)
    gate_local = gate_weight[0]
    up_local = up_weight[0]
    down_local = down_weight[0]
    contract_rows = (((0,), (0,)), ((), ()))
    contract_cols = (((1,), (1,)), ((), ()))
    gate_value = jnp.dot(expert_rows, gate_local, preferred_element_type=jnp.float32)
    up_value = jnp.dot(expert_rows, up_local, preferred_element_type=jnp.float32)
    sigmoid_gate = jax.nn.sigmoid(gate_value)
    silu_gate = gate_value * sigmoid_gate
    hidden = (silu_gate * up_value).astype(jnp.bfloat16)
    hidden_grad = lax.dot_general(
        grad_rows, down_local, contract_cols, preferred_element_type=jnp.float32
    )
    gate_grad = (
        hidden_grad * up_value * (sigmoid_gate * (1.0 + gate_value * (1.0 - sigmoid_gate)))
    ).astype(jnp.bfloat16)
    up_grad = (hidden_grad * silu_gate).astype(jnp.bfloat16)
    row_partial = lax.dot_general(
        gate_grad, gate_local, contract_cols, preferred_element_type=jnp.float32
    ) + lax.dot_general(up_grad, up_local, contract_cols, preferred_element_type=jnp.float32)
    shaped_partial = row_partial.reshape(device_count, capacity, model_width)
    returned = lax.all_to_all(
        shaped_partial.astype(jnp.bfloat16), ("ctx", "exp"), split_axis=0, concat_axis=0, tiled=True
    ).astype(shaped_partial.dtype)
    row_grads = (
        jnp.sum(returned.reshape(expert_count, 2, capacity, model_width), axis=1)
        .astype(jnp.bfloat16)
        .reshape(expert_count * capacity, model_width)
    )
    grad_down = lax.dot_general(
        hidden, grad_rows, contract_rows, preferred_element_type=jnp.float32
    ).astype(jnp.bfloat16)
    grad_gate = lax.dot_general(
        expert_rows, gate_grad, contract_rows, preferred_element_type=jnp.float32
    ).astype(jnp.bfloat16)
    grad_up = lax.dot_general(
        expert_rows, up_grad, contract_rows, preferred_element_type=jnp.float32
    ).astype(jnp.bfloat16)
    moe_grad = lax.dot_general(
        dispatch, row_grads, contract_rows, preferred_element_type=jnp.float32
    )
    token_grad = (out_grad.astype(jnp.float32) + moe_grad).astype(jnp.bfloat16)
    head_grad = lax.all_to_all(token_grad, "exp", split_axis=1, concat_axis=0, tiled=True)
    attended_grad = head_grad.reshape(block_len, head_count, head_size)
    local_grad = scaling * jnp.einsum(
        "thi,thj->hij", query, attended_grad, preferred_element_type=jnp.float32
    )
    grad_states = carried_in(local_grad, "ctx", add_states, jnp.zeros_like(local_grad))
    back_scores = jnp.einsum(
        "thd,shd->hts", attended_grad, value_heads, preferred_element_type=jnp.float32
    )
    back_scores = jnp.where(causal, back_scores, 0.0).astype(jnp.bfloat16)
    grad_f = attended_grad.astype(jnp.float32)
    grad_query = scaling * (
        jnp.einsum("hts,shd->thd", back_scores, masked_keys, preferred_element_type=jnp.float32)
        + jnp.einsum("thj,hij->thi", grad_f, states_in, precision=highest)
    )
    grad_key = spike_gate.astype(jnp.float32) * (
        scaling * jnp.einsum("hts,thd->shd", back_scores, query, preferred_element_type=jnp.float32)
        + jnp.einsum(
            "shj,hij->shi", value_heads.astype(jnp.float32), grad_states, precision=highest
        )
    )
    grad_value = scaling * jnp.einsum(
        "hts,thd->shd", scores, attended_grad, preferred_element_type=jnp.float32
    ) + jnp.einsum("shi,hij->shj", masked_keys.astype(jnp.float32), grad_states, precision=highest)
    return (
        grad_query.astype(jnp.bfloat16).reshape(block_len, local_width),
        grad_key.astype(jnp.bfloat16).reshape(block_len, local_width),
        grad_value.astype(jnp.bfloat16).reshape(block_len, local_width),
        grad_gate[None],
        grad_up[None],
        grad_down[None],
    )


def solution(mesh):
    in_specs = (
        P("ctx", "exp"),
        P("ctx", "exp"),
        P("ctx", "exp"),
        P("ctx", "exp"),
        P(("ctx", "exp"), None),
        P(("ctx", "exp"), None),
        P(("ctx", "exp"), None, None),
        P(("ctx", "exp"), None, None),
        P(("ctx", "exp"), None, None),
        P(("ctx", "exp"), None),
    )
    out_specs = (
        P("ctx", "exp"),
        P("ctx", "exp"),
        P("ctx", "exp"),
        P(("ctx", "exp"), None, None),
        P(("ctx", "exp"), None, None),
        P(("ctx", "exp"), None, None),
    )
    return jax.shard_map(
        on_device, mesh=mesh, in_specs=in_specs, out_specs=out_specs, check_vma=False
    )
```

profile of v0, /device:TPU:1, one launch (start us, length us, event | category | flops | bytes accessed | tf_op | source)
XLA Modules:
  0.0 715.0 jit_solution(378982349039709922)
XLA Ops:
  8.1 3.7 fusion.28
  13.3 3.0 fusion
  16.3 2.0 copy-done.4
  18.3 2.8 fusion.30
  21.1 67.2 %all-gather.5.cloned.1.call-done = f32[256,128,128]{2,1,0:T(8,128)} async-done(((f32[8,128,128]{2,1,0:T(8,128)}), f32[256,128,128]{2,1,0:T(8,128)}) %all-gather.5.cloned.1.call-update) | async-done | bytes 16777232 | tf_op jit(solution)/shard_map/all_gather | solution.py:11
  89.1 2.1 while.22
  89.1 2.0 bitcast_add_fusion.4
  91.1 3.2 fusion.17
  94.3 1.6 copy.164
  96.0 2.3 all_to_all.36
  98.3 4.2 all-to-all-start.1
  102.9 3.9 convolution_convert_fusion.4
  106.8 5.7 broadcast_in_dim.64
  112.5 4.2 all-to-all-done.1
  116.6 6.5 broadcast_in_dim.65
  123.1 66.9 %all-to-all-start = ((bf16[128,6,4096]{2,1,0:T(8,128)(2,1)}), bf16[128,6,4096]{2,1,0:T(8,128)(2,1)}, u32[]{:S(2)}, u32[]{:S(2)}) async-start(bf16[128,6,4096]{2,1,0:T(8,128)(2,1)} %bitcast.185), calls=%async_computation | async-start | bytes 16777216 | tf_op jit(solution)/shard_map/all_to_all | solution.py:113
  190.1 2.3 copy.165
  192.4 3.9 convolution_convert_fusion.3
  196.2 5.7 broadcast_in_dim.67
  201.9 91.7 %all-to-all-done = bf16[128,6,4096]{2,1,0:T(8,128)(2,1)} async-done(((bf16[128,6,4096]{2,1,0:T(8,128)(2,1)}), bf16[128,6,4096]{2,1,0:T(8,128)(2,1)}, u32[]{:S(2)}, u32[]{:S(2)}) %all-to-all-start) | async-done | bytes 6291488 | tf_op jit(solution)/shard_map/all_to_all | solution.py:113
  293.5 6.5 broadcast_in_dim.68
  300.1 6.4 all-to-all-start.2
  306.5 10.2 %reshape.125 = bf16[768,4096]{1,0:T(8,128)(2,1)} reshape(bf16[128,6,4096]{2,1,0:T(8,128)(2,1)} %all-to-all-done) | data formatting | bytes 12582912 | tf_op jit(solution)/shard_map/reshape | solution.py:116
  316.7 93.7 %all-to-all-done.2 = bf16[128,6,4096]{2,1,0:T(8,128)(2,1)} async-done(((bf16[128,6,4096]{2,1,0:T(8,128)(2,1)}), bf16[128,6,4096]{2,1,0:T(8,128)(2,1)}, u32[]{:S(2)}, u32[]{:S(2)}) %all-to-all-start.2) | async-done | bytes 6291488 | tf_op jit(solution)/shard_map/all_to_all | solution.py:112
  410.5 10.2 %reshape.129 = bf16[768,4096]{1,0:T(8,128)(2,1)} reshape(bf16[128,6,4096]{2,1,0:T(8,128)(2,1)} %all-to-all-done.2) | data formatting | bytes 12582912 | tf_op jit(solution)/shard_map/reshape | solution.py:115
  420.7 6.0 fusion.7
  426.7 3.4 fusion.10
  430.2 3.7 multiply_convert_fusion.2
  434.0 6.4 fusion.5
  440.4 8.3 %add_convert_fusion = bf16[768,4096]{1,0:T(8,128)(2,1)} fusion(f32[768,4096]{1,0:T(8,128)} %fusion.5, bf16[768,384]{1,0:T(8,128)(2,1)S(1)} %get-tuple-element.145, bf16[1,4096,384]{2,1,0:T(8,128)(2,1)S(1)} %copy-done.14), kind=kOutput, calls=%fused_computation.2 | convolution fusion | flops 2422210560 | bytes 22609920 | tf_op jit(solution)/shard_map/dot_general | solution.py:136
  448.7 10.2 %convert_element_type.128 = bf16[128,6,4096]{2,1,0:T(8,128)(2,1)} reshape(bf16[768,4096]{1,0:T(8,128)(2,1)} %add_convert_fusion) | data formatting | bytes 12582912 | tf_op jit(solution)/shard_map/convert_element_type | solution.py:139
  458.8 115.3 %all_to_all.50 = bf16[128,6,4096]{2,1,0:T(8,128)(2,1)} all-to-all(bf16[128,6,4096]{2,1,0:T(8,128)(2,1)} %convert_element_type.128), channel_id=1, replica_groups=mesh['ctx'=32,'exp'=4] {'ctx','exp'}, dimensions={0} | all-to-all | bytes 12582912 | tf_op jit(solution)/shard_map/all_to_all | solution.py:138
  574.2 8.7 %bitcast_reduce_fusion = bf16[64,6,4096]{2,1,0:T(8,128)(2,1)} fusion(bf16[128,6,4096]{2,1,0:T(8,128)(2,1)} %all_to_all.50), kind=kLoop, calls=%fused_computation.3 | loop fusion | flops 1572864 | bytes 9437184 | tf_op jit(solution)/shard_map/reduce_sum | solution.py:142
  582.9 4.2 convert_element_type.130
  587.0 2.0 fusion.4
  589.1 17.0 %all_to_all.51 = bf16[128,4,1024]{2,0,1:T(8,128)(2,1)S(1)} all-to-all(bf16[128,4,1024]{2,0,1:T(8,128)(2,1)S(1)} %bitcast.191), channel_id=1, replica_groups=mesh['ctx'=32,'exp'=4] {'exp'}, dimensions={1} | all-to-all | bytes 2097152 | tf_op jit(solution)/shard_map/all_to_all | solution.py:159
  610.4 8.2 %fusion.2 = bf16[1,4096,384]{2,1,0:T(8,128)(2,1)} fusion(bf16[768,4096]{1,0:T(8,128)(2,1)} %reshape.129, bf16[768,384]{1,0:T(8,128)(2,1)} %copy-done.17), kind=kOutput, calls=%fused_computation.13 | convolution fusion | flops 2417491968 | bytes 10027008 | tf_op jit(solution)/shard_map/dot_general | solution.py:152
  618.6 8.1 %fusion.1 = bf16[1,4096,384]{2,1,0:T(8,128)(2,1)} fusion(bf16[768,4096]{1,0:T(8,128)(2,1)} %reshape.129, bf16[768,384]{1,0:T(8,128)(2,1)S(1)} %copy-done.16), kind=kOutput, calls=%fused_computation.12 | convolution fusion | flops 2417491968 | bytes 10027008 | tf_op jit(solution)/shard_map/dot_general | solution.py:149
  626.7 4.2 fusion.3
  632.3 2.0 fusion.40
  636.8 5.1 fusion.51
  641.9 2.9 fusion.21
  644.8 16.8 %all-gather.7.cloned.1.call-done = bf16[256,128,128]{2,1,0:T(8,128)(2,1)} async-done(((bf16[8,128,128]{2,1,0:T(8,128)(2,1)}), bf16[256,128,128]{2,1,0:T(8,128)(2,1)}) %all-gather.7.cloned.1.call-update) | async-done | bytes 8388624 | tf_op jit(solution)/shard_map/all_gather | solution.py:24
  661.6 32.8 %while.23 = (s32[]{:T(128)}, f32[8,128,128]{2,1,0:T(8,128)S(1)}, s32[]{:T(128)}, bf16[32,8,128,128]{3,2,1,0:T(8,128)(2,1)}, s32[]{:T(128)}, /*index=5*/s32[]{:T(128)}, s32[]{:T(128)}, s32[]{:T(128)}) while((s32[]{:T(128)}, f32[8,128,128]{2,1,0:T(8,128)S(1)}, s32[]{:T(128)}, bf16[32,8,128,128]{3,2,1,0:T(8,128)(2,1)}, s32[]{:T(128)}, ...), condition=%wide.region_9.10_spmd, body=%wide.region_8.9_spmd.sunk | while | flops 262150 | bytes 1310863 | solution.py:31
  695.2 3.9 add_convert_fusion.1
  699.1 2.3 copy.184
  701.4 4.3 fusion.15
  705.7 2.3 copy.183
  (122 shorter events, 44.6 us)
Async XLA Ops:
  7.2 413.5 %copy-start = (bf16[1,4096,384]{2,1,0:T(8,128)(2,1)S(1)}, bf16[1,4096,384]{2,1,0:T(8,128)(2,1)}, u32[]{:S(2)}) copy-start(bf16[1,4096,384]{2,1,0:T(8,128)(2,1)} %param.20) | copy-start | bytes 9437188
  7.2 4.7 copy-start.19
  7.2 5.1 copy-start.21
  7.2 81.0 %all-gather.5.cloned.1.call-start = ((), (), s32[]{:S(2)}) async-start(), calls=%async_computation.5 | async-start | bytes 17301504 | tf_op jit(solution)/shard_map/all_gather | solution.py:11
  13.1 3.1 copy-start.18
  13.2 5.0 copy-start.11
  16.3 2.0 copy-start.4
  94.3 8.2 %slice-start.4 = ((s32[64,3]{0,1:T(4,128)}), s32[64,2]{0,1:T(2,128)S(1)}, s32[]{:S(2)}) async-start(s32[64,3]{0,1:T(4,128)} %copy-done.18), calls=%async_computation.11 | async-start | bytes 2048 | tf_op jit(solution)/shard_map/slice.1
  98.3 18.4 %all-to-all-start.1 = ((bf16[4,128,1024]{2,1,0:T(8,128)(2,1)}), bf16[4,128,1024]{2,1,0:T(8,128)(2,1)}, u32[]{:S(2)}, u32[]{:S(2)}) async-start(bf16[4,128,1024]{2,1,0:T(8,128)(2,1)} %all_to_all.36), calls=%async_computation.1 | async-start | bytes 2097152 | tf_op jit(solution)/shard_map/all_to_all | solution.py:80
  123.1 170.4 %all-to-all-start = ((bf16[128,6,4096]{2,1,0:T(8,128)(2,1)}), bf16[128,6,4096]{2,1,0:T(8,128)(2,1)}, u32[]{:S(2)}, u32[]{:S(2)}) async-start(bf16[128,6,4096]{2,1,0:T(8,128)(2,1)} %bitcast.185), calls=%async_computation | async-start | bytes 16777216 | tf_op jit(solution)/shard_map/all_to_all | solution.py:113
  300.1 110.4 %all-to-all-start.2 = ((bf16[128,6,4096]{2,1,0:T(8,128)(2,1)}), bf16[128,6,4096]{2,1,0:T(8,128)(2,1)}, u32[]{:S(2)}, u32[]{:S(2)}) async-start(bf16[128,6,4096]{2,1,0:T(8,128)(2,1)} %bitcast.186), calls=%async_computation.2 | async-start | bytes 16777216 | tf_op jit(solution)/shard_map/all_to_all | solution.py:112
  306.5 355.1 %all-gather.7.cloned.1.call-start = ((), (), s32[]{:S(2)}) async-start(), calls=%async_computation.6 | async-start | bytes 8650752 | tf_op jit(solution)/shard_map/all_gather | solution.py:24
  420.7 6.0 copy-start.8
  420.7 6.0 copy-start.14
  420.7 9.5 %slice-start = ((s8[6291456]{0:T(1024)(128)(4,1)}), s8[4194304]{0:T(1024)(128)(4,1)S(1)}, s32[]{:S(2)}) async-start(s8[6291456]{0:T(1024)(128)(4,1)} %bitcast.187), calls=%async_computation.7 | async-start | bytes 8388608
  426.7 3.5 copy-start.22
  426.7 3.5 slice-start.1
  426.7 3.5 copy-start.20
  430.2 3.8 copy-start.24
  434.0 6.4 copy-start.15
  434.0 6.4 copy-start.17
  589.1 19.9 %copy-start.9 = (bf16[512,1024]{1,0:T(8,128)(2,1)S(1)}, bf16[512,1024]{1,0:T(8,128)(2,1)}, u32[]{:S(2)}) copy-start(bf16[512,1024]{1,0:T(8,128)(2,1)} %param.14) | copy-start | bytes 3145732
  610.4 8.2 %copy-start.16 = (bf16[768,384]{1,0:T(8,128)(2,1)S(1)}, bf16[768,384]{1,0:T(8,128)(2,1)}, u32[]{:S(2)}) copy-start(bf16[768,384]{1,0:T(8,128)(2,1)} %copy-done.15) | copy-start | bytes 1769476
  610.4 16.3 %slice-start.2 = ((s8[6291456]{0:T(1024)(128)(4,1)}), s8[4194304]{0:T(1024)(128)(4,1)S(1)}, s32[]{:S(2)}) async-start(s8[6291456]{0:T(1024)(128)(4,1)} %bitcast.189), calls=%async_computation.9 | async-start | bytes 8388608
  618.5 8.1 %slice-start.3 = ((s8[6291456]{0:T(1024)(128)(4,1)}), s8[2097152]{0:T(1024)(128)(4,1)S(1)}, s32[]{:S(2)}) async-start(s8[6291456]{0:T(1024)(128)(4,1)} %bitcast.189), calls=%async_computation.10 | async-start | bytes 4194304
  618.6 8.1 %copy-start.23 = (f32[768,384]{1,0:T(8,128)S(1)}, f32[768,384]{1,0:T(8,128)}, u32[]{:S(2)}) copy-start(f32[768,384]{1,0:T(8,128)} %copy-done.22) | copy-start | bytes 3538948
  618.6 8.2 %copy-start.25 = (f32[768,384]{1,0:T(8,128)S(1)}, f32[768,384]{1,0:T(8,128)}, u32[]{:S(2)}) copy-start(f32[768,384]{1,0:T(8,128)} %copy-done.24) | copy-start | bytes 3538948
  626.7 4.2 copy-start.12
  630.9 1.3 copy-start.13
  632.3 2.1 copy-start.5
  632.3 2.1 copy-start.3
  636.8 5.1 copy-start.6
  636.8 5.1 copy-start.10
  641.9 53.3 %copy-start.7 = (f32[8,128,512]{2,1,0:T(8,128)S(1)}, f32[8,128,512]{2,1,0:T(8,128)}, u32[]{:S(2)}) copy-start(f32[8,128,512]{2,1,0:T(8,128)} %fusion.51) | copy-start | bytes 6291460
  694.4 0.8 copy-start.2
  701.4 6.6 copy-start.1
Sparse Core Ops, SparseCore 0:
  12.0 76.2 all-gather.4
  610.5 51.0 all-gather.6
where the time goes:
time: 720 us; the launch traced here: 715 us
  waiting for transfers between devices  274 us (38%)
  blocking collectives  132 us (18%)
  matrix products  91.8 us (13%)
  local copies, waits for them, and re-layouts  79.5 us (11%)
  starting transfers between devices  77.7 us (11%)
  other arithmetic  44.7 us (6%)
  between operations  14.8 us (2%)
    all_to_all x1, blocking collectives, on_device(): lax.all_to_all(shaped_partial.astype(jnp.bfloat16), ('ctx', 'exp'), split...  115 us
    all_to_all x1, waiting for transfers between devices, on_device(): lax.all_to_all(row_copies, ('ctx', 'exp'), split_axis=0, concat_axis=0, t...  93.7 us
    all_to_all x1, waiting for transfers between devices, on_device(): lax.all_to_all(grad_copies, ('ctx', 'exp'), split_axis=0, concat_axis=0,...  91.7 us
    all_gather x1, waiting for transfers between devices, prefix(): gathered = lax.all_gather(part, axis)  67.2 us
    all_to_all x1, starting transfers between devices, on_device(): lax.all_to_all(grad_copies, ('ctx', 'exp'), split_axis=0, concat_axis=0,...  66.9 us
    add x31, other arithmetic, add_states(): return first_part + second_part  34.1 us
    broadcast_in_dim x4, local copies, waits for them, and re-layouts, duplicate(): jnp.broadcast_to(slot_rows.reshape(expert_count, 1, capacity, model_width...  24.4 us
    all_to_all x1, blocking collectives, on_device(): lax.all_to_all(token_grad, 'exp', split_axis=1, concat_axis=0, tiled=True)  17 us
  transfers between devices with their start and end apart: 5, of which 5 were waited for; matrix products, arithmetic and copies ran while one was open for 10% of the time, Pallas kernels for 0%

commit v1 on v0

v1 whole, which is shorter than its diff:
```python
import functools
import math

import jax
import jax.numpy as jnp
from jax import lax
from jax.experimental import pallas as pl
from jax.experimental.pallas import tpu as pltpu
from jax.sharding import PartitionSpec as P

F32 = jnp.float32
BF16 = jnp.bfloat16
NN = (((1,), (0,)), ((), ()))
NT = (((1,), (1,)), ((), ()))
TN = (((0,), (0,)), ((), ()))


def mm(a, b, dims=NN):
    return lax.dot_general(a, b, dims, preferred_element_type=F32)


def call(body, grid, in_specs, out_specs, out_shape, flops, nbytes, vmem=32, **kw):
    return pl.pallas_call(
        body,
        grid=grid,
        in_specs=in_specs,
        out_specs=out_specs,
        out_shape=out_shape,
        compiler_params=pltpu.CompilerParams(
            dimension_semantics=("arbitrary",) * len(grid), vmem_limit_bytes=vmem << 20
        ),
        cost_estimate=pl.CostEstimate(
            flops=int(flops), bytes_accessed=int(nbytes), transcendentals=0
        ),
        **kw,
    )


def spike_columns(spikes, pair, width, head):
    heads = spikes.shape[1]
    col = lax.broadcasted_iota(jnp.int32, (heads, width), 1) // head + pair * (width // head)
    row = lax.broadcasted_iota(jnp.int32, (heads, width), 0)
    spread = jnp.where(col == row, 1.0, 0.0).astype(BF16)
    return mm(spikes.astype(F32).astype(BF16), spread)


def state_body(head, k_ref, v_ref, s_ref, bs_ref, mk_ref):
    width = k_ref.shape[1]
    gate = spike_columns(s_ref[...], pl.program_id(0), width, head)
    masked = (k_ref[...].astype(F32) * gate).astype(BF16)
    mk_ref[...] = masked
    value = v_ref[...]
    for h in range(width // head):
        cols = slice(h * head, (h + 1) * head)
        bs_ref[cols, :] = mm(masked[:, cols], value[:, cols], TN).astype(BF16)


def intra_body(head, q_ref, mk_ref, v_ref, o_ref):
    length, width = q_ref.shape
    t = lax.broadcasted_iota(jnp.int32, (length, length), 0)
    s = lax.broadcasted_iota(jnp.int32, (length, length), 1)
    for h in range(width // head):
        cols = slice(h * head, (h + 1) * head)
        scores = mm(q_ref[:, cols], mk_ref[:, cols], NT)
        scores = jnp.where(t >= s, scores, 0.0).astype(BF16)
        o_ref[:, cols] = mm(scores, v_ref[:, cols])


def sum_body(reverse, x_ref, o_ref):
    count = x_ref.shape[0]

    def step(i, total):
        at = count - 1 - i if reverse else i
        o_ref[at] = total.astype(BF16)
        return total + x_ref[at].astype(F32)

    lax.fori_loop(0, count, step, jnp.zeros(x_ref.shape[1:], F32))


def select_body(pack_ref, m_ref, w_ref, mt_ref):
    rows, tokens = m_ref.shape
    pack = pack_ref[0]
    first, second = pack[0:1, :], pack[1:2, :]
    place = lax.broadcasted_iota(jnp.int32, (rows, tokens), 0).astype(F32)
    hit0, hit1 = place == first, place == second
    m_ref[...] = jnp.where(hit0 | hit1, 1.0, 0.0).astype(BF16)
    w_ref[...] = jnp.where(hit0, pack[2:3, :], jnp.where(hit1, pack[3:4, :], 0.0)).astype(BF16)
    eye = lax.broadcasted_iota(jnp.int32, (tokens, tokens), 0) == lax.broadcasted_iota(
        jnp.int32, (tokens, tokens), 1
    )
    first = jnp.sum(jnp.where(eye, first, 0.0), axis=1, keepdims=True)
    second = jnp.sum(jnp.where(eye, second, 0.0), axis=1, keepdims=True)
    place = lax.broadcasted_iota(jnp.int32, (tokens, rows), 1).astype(F32)
    mt_ref[...] = jnp.where((place == first) | (place == second), 1.0, 0.0).astype(BF16)


def put_rows(m_ref, columns, o_ref):
    rows = o_ref.shape[2]
    for p in range(2):
        picked = mm(m_ref[p * rows : (p + 1) * rows, :], columns).astype(BF16)
        o_ref[p, 0] = picked
        o_ref[p, 1] = picked


def grads_body(w_ref, g_ref, o_ref):
    put_rows(w_ref, g_ref[...], o_ref)


def rows_body(head, scaling, m_ref, q_ref, intra_ref, s_ref, buf_ref, o_ref):
    del buf_ref
    width = q_ref.shape[1]
    parts = []
    for h in range(width // head):
        cols = slice(h * head, (h + 1) * head)
        inter = mm(q_ref[:, cols], s_ref[cols, :])
        parts.append((scaling * (intra_ref[:, cols] + inter)).astype(BF16))
    put_rows(m_ref, jnp.concatenate(parts, axis=1), o_ref)


def expert_body(
    steps, chunk, r_ref, g_ref, wg_ref, wu_ref, wd_ref,
    ret_ref, h_ref, gg_ref, ug_ref, gate, up, hid,
):
    i = pl.program_id(0)
    count = r_ref.shape[0] // chunk

    @pl.when(i == 0)
    def _():
        gate[...] = jnp.zeros_like(gate)
        up[...] = jnp.zeros_like(up)
        hid[...] = jnp.zeros_like(hid)

    @pl.when(i < steps)
    def _():
        @pl.loop(0, count)
        def _(c):
            rows = pl.ds(pl.multiple_of(c * chunk, chunk), chunk)
            x = r_ref[rows, :]
            gate[rows, :] += mm(x, wg_ref[...])
            up[rows, :] += mm(x, wu_ref[...])
            hid[rows, :] += mm(g_ref[rows, :], wd_ref[...], NT)

    @pl.when(i == steps - 1)
    def _():
        @pl.loop(0, count * 2)
        def _(c):
            rows = pl.ds(pl.multiple_of(c * (chunk // 2), chunk // 2), chunk // 2)
            g, u, d = gate[rows, :], up[rows, :], hid[rows, :]
            sig = jax.nn.sigmoid(g)
            silu = g * sig
            h_ref[rows, :] = (silu * u).astype(BF16)
            gg_ref[rows, :] = (d * u * (sig * (1.0 + g * (1.0 - sig)))).astype(BF16)
            ug_ref[rows, :] = (d * silu).astype(BF16)

    @pl.when(i >= steps)
    def _():
        @pl.loop(0, count)
        def _(c):
            rows = pl.ds(pl.multiple_of(c * chunk, chunk), chunk)
            ret_ref[rows, :] = (
                mm(gg_ref[rows, :], wg_ref[...], NT) + mm(ug_ref[rows, :], wu_ref[...], NT)
            ).astype(BF16)


def weights_body(r_ref, g_ref, h_ref, gg_ref, ug_ref, dg_ref, du_ref, dd_ref):
    width = r_ref.shape[1]
    chunk = 256

    @pl.loop(0, width // chunk)
    def _(c):
        cols = pl.ds(pl.multiple_of(c * chunk, chunk), chunk)
        x = r_ref[:, cols]
        dg_ref[cols, :] = mm(x, gg_ref[...], TN).astype(BF16)
        du_ref[cols, :] = mm(x, ug_ref[...], TN).astype(BF16)
        dd_ref[:, cols] = mm(h_ref[...], g_ref[:, cols], TN).astype(BF16)


def combine_body(head, scaling, mt_ref, ret_ref, og_ref, q_ref, ag_ref, lg_ref):
    width = og_ref.shape[1]
    rows = ret_ref.shape[1]
    total = og_ref[...].astype(F32)
    for p in range(2):
        both = (ret_ref[2 * p].astype(F32) + ret_ref[2 * p + 1].astype(F32)).astype(BF16)
        total = total + mm(mt_ref[:, p * rows : (p + 1) * rows], both)
    grad = total.astype(BF16)
    ag_ref[...] = grad
    for h in range(width // head):
        cols = slice(h * head, (h + 1) * head)
        lg_ref[cols, :] = (scaling * mm(q_ref[:, cols], grad[:, cols], TN)).astype(BF16)


def back_body(head, scaling, q_ref, mk_ref, v_ref, ag_ref, s_ref, gq_ref, gk_ref, gv_ref):
    length, width = q_ref.shape
    t = lax.broadcasted_iota(jnp.int32, (length, length), 0)
    s = lax.broadcasted_iota(jnp.int32, (length, length), 1)
    for h in range(width // head):
        cols = slice(h * head, (h + 1) * head)
        q, mk, v, ag = q_ref[:, cols], mk_ref[:, cols], v_ref[:, cols], ag_ref[:, cols]
        back = jnp.where(t >= s, mm(ag, v, NT), 0.0).astype(BF16)
        gq_ref[:, cols] = (scaling * (mm(back, mk) + mm(ag, s_ref[cols, :], NT))).astype(BF16)
        back = jnp.where(s >= t, mm(v, ag, NT), 0.0).astype(BF16)
        gk_ref[:, cols] = scaling * mm(back, q)
        scores = jnp.where(s >= t, mm(mk, q, NT), 0.0).astype(BF16)
        gv_ref[:, cols] = scaling * mm(scores, ag)


def final_body(head, mk_ref, v_ref, s_ref, g_ref, gki_ref, gvi_ref, gk_ref, gv_ref):
    width = mk_ref.shape[1]
    gate = spike_columns(s_ref[...], pl.program_id(0), width, head)
    for h in range(width // head):
        cols = slice(h * head, (h + 1) * head)
        state = g_ref[cols, :]
        gk = gki_ref[:, cols] + mm(v_ref[:, cols], state, NT)
        gk_ref[:, cols] = (gate[:, cols] * gk).astype(BF16)
        gv_ref[:, cols] = (gvi_ref[:, cols] + mm(mk_ref[:, cols], state)).astype(BF16)


def shape(*dims, dtype=BF16):
    return jax.ShapeDtypeStruct(dims, dtype)


def on_device(
    queries,
    key_vectors,
    value_vectors,
    spikes,
    routes,
    route_probs,
    gate_weight,
    up_weight,
    down_weight,
    out_grad,
):
    length, width = queries.shape
    heads = spikes.shape[1]
    head = width // heads
    tokens, model = out_grad.shape
    top = routes.shape[1]
    ctx = lax.axis_size("ctx")
    exp = lax.axis_size("exp")
    devices = ctx * exp
    experts = devices // 2
    capacity = 2 * max(1, 3 * tokens * top // (4 * experts))
    scaling = 1.0 / math.sqrt(head * length * ctx)
    hidden = gate_weight.shape[2]
    slots = exp * capacity
    half_rows = ctx * slots
    rows = 2 * half_rows
    pair = 2 * head
    pairs = width // pair
    everywhere = ("exp", "ctx")

    def cols(n=1, m=1):
        return pl.BlockSpec((n, m), lambda i: (0, i))

    def whole(*dims):
        return pl.BlockSpec(dims, lambda i: (0,) * len(dims))

    tall = pl.BlockSpec((pair, head), lambda i: (i, 0))
    wide = cols(length, pair)
    seq = shape(length, width)
    seq32 = shape(length, width, dtype=F32)
    unit = length * width * 2

    def exchange(part, reverse):
        pieces = part.reshape(ctx, heads * head // ctx, head)
        pieces = lax.all_to_all(pieces, "ctx", 0, 0, tiled=True)
        pieces = call(
            functools.partial(sum_body, reverse), (1,),
            [whole(*pieces.shape)], whole(*pieces.shape), shape(*pieces.shape), 1e6, 1 << 19,
        )(pieces)
        return lax.all_to_all(pieces, "ctx", 0, 0, tiled=True).reshape(heads * head, head)

    block_state, masked = call(
        functools.partial(state_body, head), (pairs,),
        [wide, wide, whole(length, heads)], [tall, wide],
        [shape(heads * head, head), seq], 2 * length * width * head, 3 * unit,
    )(key_vectors, value_vectors, spikes)
    states_in = exchange(block_state, False)
    intra = call(
        functools.partial(intra_body, head), (pairs,), [wide] * 3, wide, seq32,
        4 * length * length * width, 5 * unit,
    )(queries, masked, value_vectors)

    place = lax.broadcasted_iota(jnp.int32, (tokens, tokens), 0)
    later = place < lax.broadcasted_iota(jnp.int32, (tokens, tokens), 1)
    r0, r1 = routes[:, 0], routes[:, 1]

    def target(own):
        same = (r0[:, None] == own[None, :]).astype(jnp.int32)
        same = same + (r1[:, None] == own[None, :]).astype(jnp.int32)
        slot = jnp.sum(jnp.where(later, same, 0), axis=0)
        row = (own % 2) * half_rows + (own // 2) * slots + lax.axis_index("exp") * capacity
        return (row + slot).astype(F32)

    pack = jnp.stack(
        [target(r0), target(r1), route_probs[:, 0].astype(F32), route_probs[:, 1].astype(F32)]
    )
    pack = lax.all_gather(pack, "exp")
    select, weigh, select_t = call(
        select_body, (exp,), [pl.BlockSpec((1, 4, tokens), lambda i: (i, 0, 0))],
        [cols(rows, tokens), cols(rows, tokens), pl.BlockSpec((tokens, rows), lambda i: (i, 0))],
        [shape(rows, length), shape(rows, length), shape(length, rows)],
        1e6, 6 * rows * length,
    )(pack)

    grad_cols = lax.all_to_all(
        out_grad.reshape(tokens, exp, width).transpose(1, 0, 2), "exp", 0, 0, tiled=True
    ).reshape(length, width)
    send_shape = shape(2, 2, half_rows, 2 * width)
    send_flops = 2 * rows * length * width
    send_bytes = 4 * rows * width + 2 * rows * length + 2 * unit
    buffer = call(
        grads_body, (pairs,), [whole(rows, length), wide],
        pl.BlockSpec((2, 2, half_rows, pair), lambda i: (0, 0, 0, i + pairs)),
        send_shape, send_flops, send_bytes,
    )(weigh, grad_cols)
    buffer = call(
        functools.partial(rows_body, head, scaling), (pairs,),
        [whole(rows, length), wide, wide, tall, pl.BlockSpec(memory_space=pl.ANY)],
        pl.BlockSpec((2, 2, half_rows, pair), lambda i: (0, 0, 0, i)),
        send_shape, send_flops, send_bytes, input_output_aliases={4: 0},
    )(select, queries, intra, states_in, buffer)
    got = lax.all_to_all(
        buffer.reshape(devices, slots, 2 * width), everywhere, 0, 0, tiled=True
    ).reshape(exp * half_rows, 2 * width)

    gate_local, up_local, down_local = gate_weight[0], up_weight[0], down_weight[0]
    act = shape(half_rows, hidden)
    last = exp - 1
    block = half_rows * width * 2
    back_rows, hid, gate_grad, up_grad = call(
        functools.partial(expert_body, exp, 256), (2 * exp,),
        [
            pl.BlockSpec((half_rows, width), lambda i: (jnp.minimum(i, last), 0)),
            pl.BlockSpec((half_rows, width), lambda i: (jnp.minimum(i, last), 1)),
            pl.BlockSpec((width, hidden), lambda i: (i % exp, 0)),
            pl.BlockSpec((width, hidden), lambda i: (i % exp, 0)),
            pl.BlockSpec((hidden, width), lambda i: (0, jnp.minimum(i, last))),
        ],
        [
            pl.BlockSpec((half_rows, width), lambda i: (jnp.maximum(i - exp, 0), 0)),
            *[whole(half_rows, hidden)] * 3,
        ],
        [shape(exp * half_rows, width), act, act, act],
        10 * half_rows * model * hidden, 12 * block + 10 * model * hidden, 52,
        scratch_shapes=[pltpu.VMEM((half_rows, hidden), F32)] * 3,
    )(got, got, gate_local, up_local, down_local)
    returned = lax.all_to_all(
        back_rows.reshape(devices, slots, width), everywhere, 0, 0, tiled=True
    ).reshape(exp, half_rows, width)
    grad_gate, grad_up, grad_down = call(
        weights_body, (exp,),
        [
            pl.BlockSpec((half_rows, width), lambda i: (i, 0)),
            pl.BlockSpec((half_rows, width), lambda i: (i, 1)),
            *[whole(half_rows, hidden)] * 3,
        ],
        [
            pl.BlockSpec((width, hidden), lambda i: (i, 0)),
            pl.BlockSpec((width, hidden), lambda i: (i, 0)),
            pl.BlockSpec((hidden, width), lambda i: (0, i)),
        ],
        [shape(model, hidden), shape(model, hidden), shape(hidden, model)],
        6 * half_rows * model * hidden, 8 * block + 6 * model * hidden, 40,
    )(got, got, hid, gate_grad, up_grad)

    att_grad, local_grad = call(
        functools.partial(combine_body, head, scaling), (pairs,),
        [whole(length, rows), pl.BlockSpec((exp, half_rows, pair), lambda i: (0, 0, i)), wide, wide],
        [wide, tall], [seq, shape(heads * head, head)],
        2 * rows * length * width, 2 * rows * length + 4 * block + 3 * unit,
    )(select_t, returned, grad_cols, queries)
    grad_states = exchange(local_grad, True)
    grad_queries, keys_part, values_part = call(
        functools.partial(back_body, head, scaling), (pairs,), [wide] * 4 + [tall], [wide] * 3,
        [seq, seq32, seq32], 12 * length * length * width, 9 * unit,
    )(queries, masked, value_vectors, att_grad, states_in)
    grad_keys, grad_values = call(
        functools.partial(final_body, head), (pairs,),
        [wide, wide, whole(length, heads), tall, wide, wide], [wide] * 2, [seq, seq],
        4 * length * width * head, 8 * unit,
    )(masked, value_vectors, spikes, grad_states, keys_part, values_part)
    return grad_queries, grad_keys, grad_values, grad_gate[None], grad_up[None], grad_down[None]


def solution(mesh):
    by_head = P("ctx", "exp")
    by_device = P(("ctx", "exp"), None)
    by_half = P(("ctx", "exp"), None, None)
    return jax.shard_map(
        on_device,
        mesh=mesh,
        in_specs=(by_head,) * 4 + (by_device,) * 2 + (by_half,) * 3 + (by_device,),
        out_specs=(by_head,) * 3 + (by_half,) * 3,
        check_vma=False,
    )
```

time: 720 us -> 424 us (0.59)
  waiting for transfers between devices: 274 us -> 19.4 us
  blocking collectives: 132 us -> 248 us
  matrix products: 91.8 us -> 0 us
  Pallas kernels: 0 us -> 77.8 us
  starting transfers between devices: 77.7 us -> 32.1 us
  other arithmetic: 44.7 us -> 0.16 us
  local copies, waits for them, and re-layouts: 79.5 us -> 43.8 us
  between operations: 14.8 us -> 0.92 us
    all_to_all x3 -> x5, waiting for transfers between devices: 190 us -> 19.4 us  [the longest x1 12.7 us: on_device(): lax.all_to_all(out_grad.reshape(tokens, exp, width).transpose(1, 0, 2), '...]
    all_to_all x2, blocking collectives: 132 us -> 239 us  [the longest x1 157 us: on_device(): lax.all_to_all(buffer.reshape(devices, slots, 2 * width), everywhere, 0,...]
    dot_general x23 -> x0, matrix products: 91.8 us -> none  [the longest x1 8.3 us: on_device(): lax.dot_general(up_grad, up_local, contract_cols, preferred_element_type=...]
    all_gather x2 -> x0, waiting for transfers between devices: 84 us -> none  [the longest x1 67.2 us: prefix(): gathered = lax.all_gather(part, axis)]
    pallas_call x0 -> x12, Pallas kernels: none -> 77.8 us  [the longest x1 25.9 us: on_device(): call(functools.partial(expert_body, exp, 256), (2 * exp,), [pl.BlockSpec(...]
    all_to_all x3 -> x5, starting transfers between devices: 77.6 us -> 32.1 us  [the longest x2 15.1 us: exchange(): pieces = lax.all_to_all(pieces, 'ctx', 0, 0, tiled=True)]
    add x32 -> x0, other arithmetic: 34.2 us -> none  [the longest x31 34.1 us: add_states(): return first_part + second_part]
    unnamed x65 -> x73, local copies, waits for them, and re-layouts: 10.1 us -> 41.5 us
  transfers between devices with their start and end apart: 5 -> 5, of which waited for: 5 -> 2; matrix products, arithmetic and copies ran while one was open for 10% -> 1% of each run, Pallas kernels for 0% -> 8%
where the time goes in v1:
time: 424 us; the launch traced here: 422 us
  blocking collectives  248 us (58%)
  Pallas kernels  77.8 us (18%)
  local copies, waits for them, and re-layouts  43.8 us (10%)
  starting transfers between devices  32.1 us (8%)
  waiting for transfers between devices  19.4 us (5%)
    all_to_all x1, blocking collectives, on_device(): lax.all_to_all(buffer.reshape(devices, slots, 2 * width), everywhere, 0,...  157 us
    all_to_all x1, blocking collectives, on_device(): lax.all_to_all(back_rows.reshape(devices, slots, width), everywhere, 0, 0...  82.5 us
    unnamed x73, local copies, waits for them, and re-layouts  41.5 us
    pallas_call x1, Pallas kernels, on_device(): call(functools.partial(expert_body, exp, 256), (2 * exp,), [pl.BlockSpec(...  25.9 us
    all_to_all x2, starting transfers between devices, exchange(): pieces = lax.all_to_all(pieces, 'ctx', 0, 0, tiled=True)  15.1 us
    pallas_call x1, Pallas kernels, on_device(): call(weights_body, (exp,), [pl.BlockSpec((half_rows, width), lambda i: (i...  14.7 us
    all_to_all x2, starting transfers between devices, exchange(): lax.all_to_all(pieces, 'ctx', 0, 0, tiled=True).reshape(heads * head, head)  13 us
    all_to_all x1, waiting for transfers between devices, on_device(): lax.all_to_all(out_grad.reshape(tokens, exp, width).transpose(1, 0, 2), '...  12.7 us
  transfers between devices with their start and end apart: 5, of which 2 were waited for; matrix products, arithmetic and copies ran while one was open for 1% of the time, Pallas kernels for 8%

profile of v1, /device:TPU:1, one launch (start us, length us, event | category | flops | bytes accessed | tf_op | source)
XLA Modules:
  0.0 422.1 jit_solution(11178899700221694781)
XLA Ops:
  0.6 0.8 copy.23.s_ref
  1.5 1.2 copy-done.4
  2.7 1.2 copy-done.19
  3.9 2.5 shard_map.145
  6.4 1.0 copy-done.8
  7.4 0.7 copy-done.31
  8.1 9.7 %all-to-all-start = ((bf16[32,32,128]{2,1,0:T(8,128)(2,1)}), bf16[32,32,128]{2,1,0:T(8,128)(2,1)S(1)}, u32[]{:S(2)}, u32[]{:S(2)}) async-start(bf16[32,32,128]{2,1,0:T(8,128)(2,1)} %bitcast.77), calls=%async_computation | async-start | bytes 524288 | tf_op jit(solution)/shard_map/all_to_all | solution.py:267
  17.8 2.3 copy.28
  20.1 6.7 %all-to-all-done.x_ref = bf16[32,32,128]{2,1,0:T(8,128)(2,1)S(1)} async-done(((bf16[32,32,128]{2,1,0:T(8,128)(2,1)}), bf16[32,32,128]{2,1,0:T(8,128)(2,1)S(1)}, u32[]{:S(2)}, u32[]{:S(2)}) %all-to-all-start) | async-done | bytes 262176 | tf_op jit(solution)/shard_map/all_to_all | solution.py:267
  26.8 0.7 copy-done.20
  27.5 4.0 all-to-all-start.2
  31.7 0.9 copy-done.21
  32.9 0.7 copy-done.22
  33.6 12.7 %all-to-all-done.2 = bf16[4,128,1024]{2,1,0:T(8,128)(2,1)S(1)} async-done(((bf16[4,128,1024]{2,1,0:T(8,128)(2,1)}), bf16[4,128,1024]{2,1,0:T(8,128)(2,1)S(1)}, u32[]{:S(2)}, u32[]{:S(2)}) %all-to-all-start.2) | async-done | bytes 1048608 | tf_op jit(solution)/shard_map/all_to_all | solution.py:307
  46.3 5.5 %all-to-all-start.1 = ((bf16[32,32,128]{2,1,0:T(8,128)(2,1)}), bf16[32,32,128]{2,1,0:T(8,128)(2,1)}, u32[]{:S(2)}, u32[]{:S(2)}) async-start(bf16[32,32,128]{2,1,0:T(8,128)(2,1)} %copy-done.22), calls=%async_computation.1 | async-start | bytes 524288 | tf_op jit(solution)/shard_map/all_to_all | solution.py:272
  51.8 8.9 %all-gather.1.pack_ref = f32[4,4,128]{2,1,0:T(4,128)S(1)} all-gather(f32[1,4,128]{2,1,0:T(4,128)S(1)} %maximum_bitcast_fusion), channel_id=2, replica_groups=mesh['ctx'=32,'exp'=4] {'exp'}, dimensions={0}, use_global_device_ids=true | all-gather | bytes 10240 | tf_op jit(solution)/shard_map/all_gather | solution.py:299
  60.7 2.5 shard_map.146
  63.2 1.1 copy-done.15
  64.3 1.1 copy-done.17
  65.5 1.2 copy-done.9
  66.7 3.8 shard_map.147.intra_ref
  70.6 1.3 copy-done.6
  71.9 3.3 shard_map.149.buf_ref
  75.2 4.6 %copy-done.1 = bf16[2,2,768,2048]{3,2,1,0:T(8,128)(2,1)} copy-done((bf16[2,2,768,2048]{3,2,1,0:T(8,128)(2,1)}, bf16[2,2,768,2048]{3,2,1,0:T(8,128)(2,1)S(1)}, u32[]{:S(2)}) %copy-start.1) | copy-done | bytes 12582936
  79.7 4.6 %copy-done.2 = bf16[2,2,768,2048]{3,2,1,0:T(8,128)(2,1)S(1)} copy-done((bf16[2,2,768,2048]{3,2,1,0:T(8,128)(2,1)S(1)}, bf16[2,2,768,2048]{3,2,1,0:T(8,128)(2,1)}, u32[]{:S(2)}) %copy-start.2) | copy-done | bytes 12582936
  84.3 1.6 copy-done.7
  85.9 1.4 copy-done.16
  87.3 4.8 %shard_map.150 = bf16[2,2,768,2048]{3,2,1,0:T(8,128)(2,1)S(1)} custom-call(bf16[1536,512]{1,0:T(8,128)(2,1)S(1)} %copy-done.16, bf16[512,1024]{1,0:T(8,128)(2,1)S(1)} %copy-done.3, f32[512,1024]{1,0:T(8,128)S(1)} %copy-done.7, bf16[1024,128]{1,0:T(8,128)(2,1)} %bitcast.10.s_ref, bf16[2,2,768,2048]{3,2,1,0:T(8,128)(2,1)S(1)} %copy-done.2), custom_call_target="tpu_custom_call", output_to_operand_aliasing={{}: (4, {})} | custom-call | flops 1610612736 | bytes 9961472 | tf_op jit(solution)/shard_map/pallas_call | solution.py:318
  92.1 156.5 %all_to_all.35 = bf16[128,24,2048]{2,1,0:T(8,128)(2,1)} all-to-all(bf16[128,24,2048]{2,1,0:T(8,128)(2,1)S(1)} %bitcast.72), channel_id=1, replica_groups=mesh['ctx'=32,'exp'=4] {'exp','ctx'}, dimensions={0} | all-to-all | bytes 25165824 | tf_op jit(solution)/shard_map/all_to_all | solution.py:324
  248.7 25.9 %shard_map.151 = (bf16[3072,1024]{1,0:T(8,128)(2,1)}, bf16[768,384]{1,0:T(8,128)(2,1)S(1)}, bf16[768,384]{1,0:T(8,128)(2,1)S(1)}, bf16[768,384]{1,0:T(8,128)(2,1)S(1)}) custom-call(bf16[3072,2048]{1,0:T(8,128)(2,1)} %bitcast.68, bf16[3072,2048]{1,0:T(8,128)(2,1)} %bitcast.69, bf16[4096,384]{1,0:T(8,128)(2,1)} %bitcast.81, bf16[4096,384]{1,0:T(8,128)(2,1)} %bitcast.82, ...), custom_call_target="tpu_custom_call" | custom-call | flops 12079595520 | bytes 34603008 | tf_op jit(solution)/shard_map/pallas_call | solution.py:332
  274.6 82.5 %all_to_all.36 = bf16[128,24,1024]{2,1,0:T(8,128)(2,1)S(1)} all-to-all(bf16[128,24,1024]{2,1,0:T(8,128)(2,1)} %bitcast.78), channel_id=1, replica_groups=mesh['ctx'=32,'exp'=4] {'exp','ctx'}, dimensions={0} | all-to-all | bytes 12582912 | tf_op jit(solution)/shard_map/all_to_all | solution.py:349
  357.1 4.8 %shard_map.152 = (bf16[512,1024]{1,0:T(8,128)(2,1)S(1)}, bf16[1024,128]{1,0:T(8,128)(2,1)S(1)}) custom-call(bf16[512,1536]{1,0:T(8,128)(2,1)S(1)} %copy-done.18, bf16[4,768,1024]{2,1,0:T(8,128)(2,1)S(1)} %bitcast.73, bf16[512,1024]{1,0:T(8,128)(2,1)S(1)} %bitcast.75, bf16[512,1024]{1,0:T(8,128)(2,1)S(1)} %copy-done.3), custom_call_target="tpu_custom_call" | custom-call | flops 1610612736 | bytes 11010048 | tf_op jit(solution)/shard_map/pallas_call | solution.py:368
  362.7 1.0 copy-done.32
  363.6 5.3 %all-to-all-start.5 = ((bf16[32,32,128]{2,1,0:T(8,128)(2,1)}), bf16[32,32,128]{2,1,0:T(8,128)(2,1)}, u32[]{:S(2)}, u32[]{:S(2)}) async-start(bf16[32,32,128]{2,1,0:T(8,128)(2,1)} %bitcast.76), calls=%async_computation.5 | async-start | bytes 524288 | tf_op jit(solution)/shard_map/all_to_all | solution.py:267
  369.0 4.6 %copy-done = bf16[128,24,2048]{2,1,0:T(8,128)(2,1)S(1)} copy-done((bf16[128,24,2048]{2,1,0:T(8,128)(2,1)S(1)}, bf16[128,24,2048]{2,1,0:T(8,128)(2,1)}, u32[]{:S(2)}) %copy-start) | copy-done | bytes 12582936
  373.6 1.1 copy-done.25
  374.6 1.1 copy-done.27
  375.7 1.1 copy-done.29
  376.8 14.7 %shard_map.156 = (bf16[4096,384]{1,0:T(8,128)(2,1)}, bf16[4096,384]{1,0:T(8,128)(2,1)}, bf16[384,4096]{1,0:T(8,128)(2,1)}) custom-call(bf16[3072,2048]{1,0:T(8,128)(2,1)S(1)} %bitcast.70, bf16[3072,2048]{1,0:T(8,128)(2,1)S(1)} %bitcast.71, bf16[768,384]{1,0:T(8,128)(2,1)S(1)} %copy-done.25, bf16[768,384]{1,0:T(8,128)(2,1)S(1)} %copy-done.27, ...), custom_call_target="tpu_custom_call" | custom-call | flops 7247757312 | bytes 22020096 | tf_op jit(solution)/shard_map/pallas_call | solution.py:352
  391.5 1.1 shard_map.154
  393.3 7.6 %all-to-all-start.6 = ((bf16[32,32,128]{2,1,0:T(8,128)(2,1)}), bf16[32,32,128]{2,1,0:T(8,128)(2,1)}, u32[]{:S(2)}, u32[]{:S(2)}) async-start(bf16[32,32,128]{2,1,0:T(8,128)(2,1)} %copy-done.23), calls=%async_computation.6 | async-start | bytes 524288 | tf_op jit(solution)/shard_map/all_to_all | solution.py:272
  400.9 1.2 copy-done.33
  402.1 10.1 %shard_map.153 = (bf16[512,1024]{1,0:T(8,128)(2,1)}, f32[512,1024]{1,0:T(8,128)S(1)}, f32[512,1024]{1,0:T(8,128)S(1)}) custom-call(bf16[512,1024]{1,0:T(8,128)(2,1)S(1)} %copy-done.3, bf16[512,1024]{1,0:T(8,128)(2,1)S(1)} %copy-done.10, bf16[512,1024]{1,0:T(8,128)(2,1)S(1)} %copy-done.5, bf16[512,1024]{1,0:T(8,128)(2,1)S(1)} %copy-done.33, ...), custom_call_target="tpu_custom_call" | custom-call | flops 3221225472 | bytes 9437184 | tf_op jit(solution)/shard_map/pallas_call | solution.py:375
  412.2 1.3 copy-done.11
  413.5 1.3 copy-done.13
  414.9 1.6 copy-done.12
  416.5 1.6 copy-done.14
  418.0 4.1 shard_map.155
  (56 shorter events, 1.8 us)
Async XLA Ops:
  1.5 1.2 copy-start.4
  2.7 1.2 copy-start.19
  3.9 27.6 %copy-start.34 = (s32[128,2]{0,1:T(2,128)S(1)}, s32[128,2]{0,1:T(2,128)}, u32[]{:S(2)}) copy-start(s32[128,2]{0,1:T(2,128)} %param.14) | copy-start | bytes 3076
  3.9 27.7 %copy-start.35 = (bf16[128,2]{0,1:T(2,128)(2,1)S(1)}, bf16[128,2]{0,1:T(2,128)(2,1)}, u32[]{:S(2)}) copy-start(bf16[128,2]{0,1:T(2,128)(2,1)} %param.15) | copy-start | bytes 1540
  6.4 1.0 copy-start.8
  7.4 0.7 copy-start.31
  8.1 57.4 %copy-start.3 = (bf16[512,1024]{1,0:T(8,128)(2,1)S(1)}, bf16[512,1024]{1,0:T(8,128)(2,1)}, u32[]{:S(2)}) copy-start(bf16[512,1024]{1,0:T(8,128)(2,1)} %q_ref.7) | copy-start | bytes 3145732
  8.1 57.4 %copy-start.5 = (bf16[512,1024]{1,0:T(8,128)(2,1)S(1)}, bf16[512,1024]{1,0:T(8,128)(2,1)}, u32[]{:S(2)}) copy-start(bf16[512,1024]{1,0:T(8,128)(2,1)} %v_ref.7) | copy-start | bytes 3145732
  8.1 18.7 %all-to-all-start = ((bf16[32,32,128]{2,1,0:T(8,128)(2,1)}), bf16[32,32,128]{2,1,0:T(8,128)(2,1)S(1)}, u32[]{:S(2)}, u32[]{:S(2)}) async-start(bf16[32,32,128]{2,1,0:T(8,128)(2,1)} %bitcast.77), calls=%async_computation | async-start | bytes 524288 | tf_op jit(solution)/shard_map/all_to_all | solution.py:267
  26.8 0.7 copy-start.20
  27.5 18.7 %all-to-all-start.2 = ((bf16[4,128,1024]{2,1,0:T(8,128)(2,1)}), bf16[4,128,1024]{2,1,0:T(8,128)(2,1)S(1)}, u32[]{:S(2)}, u32[]{:S(2)}) async-start(bf16[4,128,1024]{2,1,0:T(8,128)(2,1)} %bitcast.79), calls=%async_computation.2 | async-start | bytes 2097152 | tf_op jit(solution)/shard_map/all_to_all | solution.py:307
  31.7 1.0 copy-start.21
  32.9 0.7 copy-start.22
  46.3 33.5 %all-to-all-start.1 = ((bf16[32,32,128]{2,1,0:T(8,128)(2,1)}), bf16[32,32,128]{2,1,0:T(8,128)(2,1)}, u32[]{:S(2)}, u32[]{:S(2)}) async-start(bf16[32,32,128]{2,1,0:T(8,128)(2,1)} %copy-done.22), calls=%async_computation.1 | async-start | bytes 524288 | tf_op jit(solution)/shard_map/all_to_all | solution.py:272
  63.2 1.1 copy-start.15
  64.3 1.1 copy-start.17
  65.5 1.2 copy-start.9
  70.5 1.3 copy-start.6
  75.2 4.6 %copy-start.1 = (bf16[2,2,768,2048]{3,2,1,0:T(8,128)(2,1)}, bf16[2,2,768,2048]{3,2,1,0:T(8,128)(2,1)S(1)}, u32[]{:S(2)}) copy-start(bf16[2,2,768,2048]{3,2,1,0:T(8,128)(2,1)S(1)} %shard_map.149.buf_ref) | copy-start | bytes 37748740
  79.7 4.6 %copy-start.2 = (bf16[2,2,768,2048]{3,2,1,0:T(8,128)(2,1)S(1)}, bf16[2,2,768,2048]{3,2,1,0:T(8,128)(2,1)}, u32[]{:S(2)}) copy-start(bf16[2,2,768,2048]{3,2,1,0:T(8,128)(2,1)} %copy-done.1) | copy-start | bytes 37748740
  84.3 1.6 copy-start.7
  85.9 1.4 copy-start.16
  274.6 82.5 %copy-start.24 = (bf16[768,384]{1,0:T(8,128)(2,1)}, bf16[768,384]{1,0:T(8,128)(2,1)S(1)}, u32[]{:S(2)}) copy-start(bf16[768,384]{1,0:T(8,128)(2,1)S(1)} %get-tuple-element.38.h_ref) | copy-start | bytes 1769476
  274.6 82.5 %copy-start.26 = (bf16[768,384]{1,0:T(8,128)(2,1)}, bf16[768,384]{1,0:T(8,128)(2,1)S(1)}, u32[]{:S(2)}) copy-start(bf16[768,384]{1,0:T(8,128)(2,1)S(1)} %get-tuple-element.39.gg_ref) | copy-start | bytes 1769476
  274.6 82.5 %copy-start.28 = (bf16[768,384]{1,0:T(8,128)(2,1)}, bf16[768,384]{1,0:T(8,128)(2,1)S(1)}, u32[]{:S(2)}) copy-start(bf16[768,384]{1,0:T(8,128)(2,1)S(1)} %get-tuple-element.40.ug_ref) | copy-start | bytes 1769476
  274.6 82.5 %copy-start.18 = (bf16[512,1536]{1,0:T(8,128)(2,1)S(1)}, bf16[512,1536]{1,0:T(8,128)(2,1)}, u32[]{:S(2)}) copy-start(bf16[512,1536]{1,0:T(8,128)(2,1)} %copy-done.17) | copy-start | bytes 4718596
  362.0 0.7 copy-start.30
  362.7 1.0 copy-start.32
  363.6 27.9 %all-to-all-start.5 = ((bf16[32,32,128]{2,1,0:T(8,128)(2,1)}), bf16[32,32,128]{2,1,0:T(8,128)(2,1)}, u32[]{:S(2)}, u32[]{:S(2)}) async-start(bf16[32,32,128]{2,1,0:T(8,128)(2,1)} %bitcast.76), calls=%async_computation.5 | async-start | bytes 524288 | tf_op jit(solution)/shard_map/all_to_all | solution.py:267
  369.0 4.6 %copy-start = (bf16[128,24,2048]{2,1,0:T(8,128)(2,1)S(1)}, bf16[128,24,2048]{2,1,0:T(8,128)(2,1)}, u32[]{:S(2)}) copy-start(bf16[128,24,2048]{2,1,0:T(8,128)(2,1)} %all_to_all.35) | copy-start | bytes 37748740
  373.6 1.1 copy-start.25
  374.6 1.1 copy-start.27
  375.7 1.1 copy-start.29
  376.8 24.1 %copy-start.10 = (bf16[512,1024]{1,0:T(8,128)(2,1)S(1)}, bf16[512,1024]{1,0:T(8,128)(2,1)}, u32[]{:S(2)}) copy-start(bf16[512,1024]{1,0:T(8,128)(2,1)} %copy-done.8) | copy-start | bytes 3145732
  392.6 0.7 copy-start.23
  393.3 21.6 %all-to-all-start.6 = ((bf16[32,32,128]{2,1,0:T(8,128)(2,1)}), bf16[32,32,128]{2,1,0:T(8,128)(2,1)}, u32[]{:S(2)}, u32[]{:S(2)}) async-start(bf16[32,32,128]{2,1,0:T(8,128)(2,1)} %copy-done.23), calls=%async_computation.6 | async-start | bytes 524288 | tf_op jit(solution)/shard_map/all_to_all | solution.py:272
  400.9 1.2 copy-start.33
  412.2 1.3 copy-start.11
  413.5 1.3 copy-start.13
  414.9 1.6 copy-start.12
  416.5 1.6 copy-start.14

commit v2 on v1

v2 whole, which is shorter than its diff:
```python
import functools
import math

import jax
import jax.numpy as jnp
from jax import lax
from jax.experimental import pallas as pl
from jax.experimental.pallas import tpu as pltpu
from jax.sharding import PartitionSpec as P

F32 = jnp.float32
BF16 = jnp.bfloat16
NN = (((1,), (0,)), ((), ()))
NT = (((1,), (1,)), ((), ()))
TN = (((0,), (0,)), ((), ()))


def mm(a, b, dims=NN):
    return lax.dot_general(a, b, dims, preferred_element_type=F32)


def call(body, grid, in_specs, out_specs, out_shape, flops, nbytes, vmem=60, **kw):
    return pl.pallas_call(
        body,
        grid=grid,
        in_specs=in_specs,
        out_specs=out_specs,
        out_shape=out_shape,
        compiler_params=pltpu.CompilerParams(
            dimension_semantics=("arbitrary",) * len(grid), vmem_limit_bytes=vmem << 20
        ),
        cost_estimate=pl.CostEstimate(
            flops=int(flops), bytes_accessed=int(nbytes), transcendentals=0
        ),
        **kw,
    )


def spike_columns(spikes, pair, width, head):
    heads = spikes.shape[1]
    col = lax.broadcasted_iota(jnp.int32, (heads, width), 1) // head + pair * (width // head)
    row = lax.broadcasted_iota(jnp.int32, (heads, width), 0)
    spread = jnp.where(col == row, 1.0, 0.0).astype(BF16)
    return mm(spikes.astype(F32).astype(BF16), spread)


def cut_body(capacity, slots, half_rows, mine_ref, x_ref, r_ref, p_ref, *o_refs):
    width = o_refs[0].shape[1]
    tokens = x_ref.shape[0]
    extra = o_refs[0].shape[0] - tokens
    row = lax.broadcasted_iota(jnp.int32, (tokens, tokens), 0)
    col = lax.broadcasted_iota(jnp.int32, (tokens, tokens), 1)

    def lanes(column):
        return jnp.sum(jnp.where(row == col, column, 0.0), axis=0, keepdims=True)

    named = r_ref[...].astype(F32)
    probs = p_ref[...].astype(F32)
    line = lax.broadcasted_iota(jnp.int32, (extra, tokens), 0)
    pack = jnp.zeros((extra, tokens), F32)
    for k in range(2):
        expert = lanes(named[:, k : k + 1])
        same = jnp.where(named[:, 0:1] == expert, 1.0, 0.0)
        same = same + jnp.where(named[:, 1:2] == expert, 1.0, 0.0)
        slot = jnp.sum(jnp.where(row < col, same, 0.0), axis=0, keepdims=True)
        half = jnp.floor(expert * 0.5)
        place = (expert - 2.0 * half) * half_rows + half * slots + slot
        place = place + (mine_ref[0] * capacity).astype(F32)
        high = jnp.floor(place * 0.125)
        for at, value in (
            (3 * k, high), (3 * k + 1, place - 8.0 * high), (3 * k + 2, lanes(probs[:, k : k + 1]))
        ):
            pack = jnp.where(line == at, value, pack)
    for i, o_ref in enumerate(o_refs):
        at = lax.rem(mine_ref[0] + i, len(o_refs)) * width
        o_ref[:tokens, :] = x_ref[:, pl.ds(pl.multiple_of(at, width), width)]
        o_ref[tokens:, :] = jnp.zeros((extra, width), BF16)
        o_ref[tokens:, :tokens] = pack.astype(BF16)


def prepare_body(count, mine_ref, *refs):
    x_refs, (g_ref, m_ref, mt_ref, o_ref, w_ref) = refs[:count], refs[count:]
    rows = m_ref.shape[0]
    tokens = g_ref.shape[0] // count
    pair = o_ref.shape[3]
    step = pl.program_id(0)

    @pl.when(step == 0)
    def _():
        down = lax.broadcasted_iota(jnp.int32, (rows, tokens), 0).astype(F32)
        across = lax.broadcasted_iota(jnp.int32, (tokens, rows), 1).astype(F32)
        eye = lax.broadcasted_iota(jnp.int32, (tokens, tokens), 0) == lax.broadcasted_iota(
            jnp.int32, (tokens, tokens), 1
        )
        for i, x_ref in enumerate(x_refs):
            at = pl.multiple_of(lax.rem(mine_ref[0] + count - i, count) * tokens, tokens)
            g_ref[pl.ds(at, tokens), :] = x_ref[:tokens, :]
            pack = x_ref[tokens:, :tokens].astype(F32)
            first = 8.0 * pack[0:1] + pack[1:2]
            second = 8.0 * pack[3:4] + pack[4:5]
            hit0, hit1 = down == first, down == second
            m_ref[:, pl.ds(at, tokens)] = jnp.where(hit0 | hit1, 1.0, 0.0).astype(BF16)
            w_ref[:, pl.ds(at, tokens)] = jnp.where(
                hit0, pack[2:3], jnp.where(hit1, pack[5:6], 0.0)
            ).astype(BF16)
            first = jnp.sum(jnp.where(eye, first, 0.0), axis=1, keepdims=True)
            second = jnp.sum(jnp.where(eye, second, 0.0), axis=1, keepdims=True)
            mt_ref[pl.ds(at, tokens), :] = jnp.where(
                (across == first) | (across == second), 1.0, 0.0
            ).astype(BF16)

    @pl.when(step > 0)
    def _():
        cols = pl.ds(pl.multiple_of((step - 1) * pair, pair), pair)
        put_rows(w_ref, g_ref[:, cols], o_ref)


def state_body(head, k_ref, v_ref, s_ref, bs_ref, mk_ref):
    width = k_ref.shape[1]
    gate = spike_columns(s_ref[...], pl.program_id(0), width, head)
    masked = (k_ref[...].astype(F32) * gate).astype(BF16)
    mk_ref[...] = masked
    value = v_ref[...]
    for h in range(width // head):
        cols = slice(h * head, (h + 1) * head)
        bs_ref[cols, :] = mm(masked[:, cols], value[:, cols], TN).astype(BF16)


def intra_body(head, q_ref, mk_ref, v_ref, o_ref):
    length, width = q_ref.shape
    t = lax.broadcasted_iota(jnp.int32, (length, length), 0)
    s = lax.broadcasted_iota(jnp.int32, (length, length), 1)
    for h in range(width // head):
        cols = slice(h * head, (h + 1) * head)
        scores = mm(q_ref[:, cols], mk_ref[:, cols], NT)
        scores = jnp.where(t >= s, scores, 0.0).astype(BF16)
        o_ref[:, cols] = mm(scores, v_ref[:, cols])


def sum_body(reverse, x_ref, o_ref):
    count = x_ref.shape[0]

    def step(i, total):
        at = count - 1 - i if reverse else i
        o_ref[at] = total.astype(BF16)
        return total + x_ref[at].astype(F32)

    lax.fori_loop(0, count, step, jnp.zeros(x_ref.shape[1:], F32))


def put_rows(m_ref, columns, o_ref):
    rows = o_ref.shape[2]
    for p in range(2):
        picked = mm(m_ref[p * rows : (p + 1) * rows, :], columns).astype(BF16)
        o_ref[p, 0] = picked
        o_ref[p, 1] = picked


def rows_body(head, scaling, m_ref, q_ref, intra_ref, s_ref, buf_ref, o_ref):
    del buf_ref
    width = q_ref.shape[1]
    parts = []
    for h in range(width // head):
        cols = slice(h * head, (h + 1) * head)
        inter = mm(q_ref[:, cols], s_ref[cols, :])
        parts.append((scaling * (intra_ref[:, cols] + inter)).astype(BF16))
    put_rows(m_ref, jnp.concatenate(parts, axis=1), o_ref)


def expert_body(
    steps, r_ref, g_ref, wg_ref, wu_ref, wd_ref, ret_ref, h_ref, a_ref, gate, up, hid
):
    i = pl.program_id(0)
    rows, width = hid.shape
    chunk = rows // 6

    @pl.when(i == 0)
    def _():
        gate[...] = mm(r_ref[...], wg_ref[...])
        up[...] = mm(r_ref[...], wu_ref[...])
        hid[...] = mm(g_ref[...], wd_ref[...], NT)

    @pl.when((i > 0) & (i < steps))
    def _():
        gate[...] += mm(r_ref[...], wg_ref[...])
        up[...] += mm(r_ref[...], wu_ref[...])
        hid[...] += mm(g_ref[...], wd_ref[...], NT)

    @pl.when(i == steps - 1)
    def _():
        @pl.loop(0, rows // chunk)
        def _(c):
            part = pl.ds(pl.multiple_of(c * chunk, chunk), chunk)
            g, u, d = gate[part, :], up[part, :], hid[part, :]
            sig = jax.nn.sigmoid(g)
            silu = g * sig
            h_ref[part, :] = (silu * u).astype(BF16)
            a_ref[part, :width] = (d * u * (sig * (1.0 + g * (1.0 - sig)))).astype(BF16)
            a_ref[part, width:] = (d * silu).astype(BF16)

    @pl.when(i >= steps)
    def _():
        ret_ref[...] = (
            mm(a_ref[:, :width], wg_ref[...], NT) + mm(a_ref[:, width:], wu_ref[...], NT)
        ).astype(BF16)


def weights_body(r_ref, g_ref, h_ref, a_ref, dg_ref, du_ref, dd_ref):
    width = r_ref.shape[1]
    hidden = h_ref.shape[1]
    chunk = 256

    @pl.loop(0, width // chunk)
    def _(c):
        cols = pl.ds(pl.multiple_of(c * chunk, chunk), chunk)
        both = mm(r_ref[:, cols], a_ref[...], TN)
        dg_ref[cols, :] = both[:, :hidden].astype(BF16)
        du_ref[cols, :] = both[:, hidden:].astype(BF16)
        dd_ref[:, cols] = mm(h_ref[...], g_ref[:, cols], TN).astype(BF16)


def combine_body(head, scaling, mt_ref, ret_ref, og_ref, q_ref, ag_ref, lg_ref):
    width = og_ref.shape[1]
    rows = ret_ref.shape[1]
    total = og_ref[...].astype(F32)
    for p in range(2):
        both = (ret_ref[2 * p].astype(F32) + ret_ref[2 * p + 1].astype(F32)).astype(BF16)
        total = total + mm(mt_ref[:, p * rows : (p + 1) * rows], both)
    grad = total.astype(BF16)
    ag_ref[...] = grad
    for h in range(width // head):
        cols = slice(h * head, (h + 1) * head)
        lg_ref[cols, :] = (scaling * mm(q_ref[:, cols], grad[:, cols], TN)).astype(BF16)


def back_query_body(head, scaling, mk_ref, v_ref, ag_ref, s_ref, gq_ref):
    length, width = mk_ref.shape
    t = lax.broadcasted_iota(jnp.int32, (length, length), 0)
    s = lax.broadcasted_iota(jnp.int32, (length, length), 1)
    for h in range(width // head):
        cols = slice(h * head, (h + 1) * head)
        ag = ag_ref[:, cols]
        back = jnp.where(t >= s, mm(ag, v_ref[:, cols], NT), 0.0).astype(BF16)
        total = mm(back, mk_ref[:, cols]) + mm(ag, s_ref[cols, :], NT)
        gq_ref[:, cols] = (scaling * total).astype(BF16)


def back_body(head, scaling, q_ref, mk_ref, v_ref, ag_ref, gk_ref, gv_ref):
    length, width = q_ref.shape
    s = lax.broadcasted_iota(jnp.int32, (length, length), 0)
    t = lax.broadcasted_iota(jnp.int32, (length, length), 1)
    for h in range(width // head):
        cols = slice(h * head, (h + 1) * head)
        q, ag = q_ref[:, cols], ag_ref[:, cols]
        back = jnp.where(t >= s, mm(v_ref[:, cols], ag, NT), 0.0).astype(BF16)
        gk_ref[:, cols] = scaling * mm(back, q)
        scores = jnp.where(t >= s, mm(mk_ref[:, cols], q, NT), 0.0).astype(BF16)
        gv_ref[:, cols] = scaling * mm(scores, ag)


def final_body(head, mk_ref, v_ref, s_ref, g_ref, gki_ref, gvi_ref, gk_ref, gv_ref):
    width = mk_ref.shape[1]
    gate = spike_columns(s_ref[...], pl.program_id(0), width, head)
    for h in range(width // head):
        cols = slice(h * head, (h + 1) * head)
        state = g_ref[cols, :]
        gk = gki_ref[:, cols] + mm(v_ref[:, cols], state, NT)
        gk_ref[:, cols] = (gate[:, cols] * gk).astype(BF16)
        gv_ref[:, cols] = (gvi_ref[:, cols] + mm(mk_ref[:, cols], state)).astype(BF16)


def shape(*dims, dtype=BF16):
    return jax.ShapeDtypeStruct(dims, dtype)


def on_device(
    queries,
    key_vectors,
    value_vectors,
    spikes,
    routes,
    route_probs,
    gate_weight,
    up_weight,
    down_weight,
    out_grad,
):
    length, width = queries.shape
    heads = spikes.shape[1]
    head = width // heads
    tokens, model = out_grad.shape
    top = routes.shape[1]
    ctx = lax.axis_size("ctx")
    exp = lax.axis_size("exp")
    devices = ctx * exp
    experts = devices // 2
    capacity = 2 * max(1, 3 * tokens * top // (4 * experts))
    scaling = 1.0 / math.sqrt(head * length * ctx)
    hidden = gate_weight.shape[2]
    slots = exp * capacity
    half_rows = ctx * slots
    rows = 2 * half_rows
    pair = 2 * head
    pairs = width // pair
    everywhere = ("exp", "ctx")

    def cols(n=1, m=1):
        return pl.BlockSpec((n, m), lambda i: (0, i))

    def whole(*dims):
        return pl.BlockSpec(dims, lambda i: (0,) * len(dims))

    tall = pl.BlockSpec((pair, head), lambda i: (i, 0))
    wide = cols(length, pair)
    seq = shape(length, width)
    seq32 = shape(length, width, dtype=F32)
    unit = length * width * 2

    def exchange(part, reverse, cover):
        pieces = part.reshape(ctx, heads * head // ctx, head)
        pieces = lax.all_to_all(pieces, "ctx", 0, 0, tiled=True)
        pieces, cover = lax.optimization_barrier((pieces, cover))
        pieces = call(
            functools.partial(sum_body, reverse), (1,),
            [whole(*pieces.shape)], whole(*pieces.shape), shape(*pieces.shape), 1e6, 1 << 19, 4,
        )(pieces)
        pieces = lax.all_to_all(pieces, "ctx", 0, 0, tiled=True)
        return pieces.reshape(heads * head, head), cover

    block_state, masked = call(
        functools.partial(state_body, head), (pairs,),
        [wide, wide, whole(length, heads)], [tall, wide],
        [shape(heads * head, head), seq], 2 * length * width * head, 3 * unit,
    )(key_vectors, value_vectors, spikes)
    mine = lax.axis_index("exp").reshape(1)
    smem = pl.BlockSpec(memory_space=pltpu.SMEM)
    piece = (tokens + 16, width)
    pieces = call(
        functools.partial(cut_body, capacity, slots, half_rows), (1,),
        [smem, whole(tokens, model), whole(tokens, top), whole(tokens, top)],
        [whole(*piece)] * exp, [shape(*piece)] * exp, 1e6, 2 * unit,
    )(mine, out_grad, routes, route_probs)
    pieces, block_state = lax.optimization_barrier((tuple(pieces), block_state))
    pieces = [pieces[0]] + [
        lax.ppermute(pieces[i], "exp", [(j, (j + i) % exp) for j in range(exp)])
        for i in range(1, exp)
    ]
    states_in, _ = exchange(block_state, False, ())
    intra = call(
        functools.partial(intra_body, head), (pairs,), [wide] * 3, wide, seq32,
        4 * length * length * width, 5 * unit,
    )(queries, masked, value_vectors)

    send_shape = shape(2, 2, half_rows, 2 * width)
    send_flops = 2 * rows * length * width
    send_bytes = 4 * rows * width + 2 * rows * length + 2 * unit
    grad_cols, select, select_t, buffer = call(
        functools.partial(prepare_body, exp), (1 + pairs,), [smem] + [whole(*piece)] * exp,
        [
            whole(length, width), whole(rows, length), whole(length, rows),
            pl.BlockSpec(
                (2, 2, half_rows, pair), lambda i: (0, 0, 0, jnp.maximum(i - 1, 0) + pairs)
            ),
        ],
        [seq, shape(rows, length), shape(length, rows), send_shape], send_flops, send_bytes,
        scratch_shapes=[pltpu.VMEM((rows, length), BF16)],
    )(mine, *pieces)
    buffer = call(
        functools.partial(rows_body, head, scaling), (pairs,),
        [whole(rows, length), wide, wide, tall, pl.BlockSpec(memory_space=pl.ANY)],
        pl.BlockSpec((2, 2, half_rows, pair), lambda i: (0, 0, 0, i)),
        send_shape, send_flops, send_bytes, input_output_aliases={4: 0},
    )(select, queries, intra, states_in, buffer)
    got = lax.all_to_all(
        buffer.reshape(devices, slots, 2 * width), everywhere, 0, 0, tiled=True
    ).reshape(exp * half_rows, 2 * width)

    act = shape(half_rows, hidden)
    last = exp - 1
    block = half_rows * width * 2
    back_rows, hid, acts = call(
        functools.partial(expert_body, exp), (2 * exp,),
        [
            pl.BlockSpec((half_rows, width), lambda i: (jnp.minimum(i, last), 0)),
            pl.BlockSpec((half_rows, width), lambda i: (jnp.minimum(i, last), 1)),
            pl.BlockSpec((width, hidden), lambda i: (i % exp, 0)),
            pl.BlockSpec((width, hidden), lambda i: (i % exp, 0)),
            pl.BlockSpec((hidden, width), lambda i: (0, jnp.minimum(i, last))),
        ],
        [
            pl.BlockSpec((half_rows, width), lambda i: (jnp.maximum(i - exp, 0), 0)),
            whole(half_rows, hidden),
            whole(half_rows, 2 * hidden),
        ],
        [shape(exp * half_rows, width), act, shape(half_rows, 2 * hidden)],
        10 * half_rows * model * hidden, 12 * block + 10 * model * hidden,
        scratch_shapes=[pltpu.VMEM((half_rows, hidden), F32)] * 3,
    )(got, got, gate_weight[0], up_weight[0], down_weight[0])
    returned = lax.all_to_all(
        back_rows.reshape(devices, slots, width), everywhere, 0, 0, tiled=True
    ).reshape(exp, half_rows, width)
    grad_gate, grad_up, grad_down = call(
        weights_body, (exp,),
        [
            pl.BlockSpec((half_rows, width), lambda i: (i, 0)),
            pl.BlockSpec((half_rows, width), lambda i: (i, 1)),
            whole(half_rows, hidden),
            whole(half_rows, 2 * hidden),
        ],
        [
            pl.BlockSpec((width, hidden), lambda i: (i, 0)),
            pl.BlockSpec((width, hidden), lambda i: (i, 0)),
            pl.BlockSpec((hidden, width), lambda i: (0, i)),
        ],
        [shape(model, hidden), shape(model, hidden), shape(hidden, model)],
        6 * half_rows * model * hidden, 8 * block + 6 * model * hidden,
    )(got, got, hid, acts)

    returned, grad_gate, grad_up, grad_down = lax.optimization_barrier(
        (returned, grad_gate, grad_up, grad_down)
    )

    att_grad, local_grad = call(
        functools.partial(combine_body, head, scaling), (pairs,),
        [whole(length, rows), pl.BlockSpec((exp, half_rows, pair), lambda i: (0, 0, i)), wide, wide],
        [wide, tall], [seq, shape(heads * head, head)],
        2 * rows * length * width, 2 * rows * length + 4 * block + 3 * unit,
    )(select_t, returned, grad_cols, queries)
    parts = call(
        functools.partial(back_body, head, scaling), (pairs,), [wide] * 4, [wide] * 2,
        [seq32, seq32], 8 * length * length * width, 8 * unit,
    )(queries, masked, value_vectors, att_grad)
    grad_states, (keys_part, values_part) = exchange(local_grad, True, tuple(parts))
    grad_queries = call(
        functools.partial(back_query_body, head, scaling), (pairs,), [wide] * 3 + [tall], wide, seq,
        4 * length * length * width, 4 * unit,
    )(masked, value_vectors, att_grad, states_in)
    grad_keys, grad_values = call(
        functools.partial(final_body, head), (pairs,),
        [wide, wide, whole(length, heads), tall, wide, wide], [wide] * 2, [seq, seq],
        4 * length * width * head, 8 * unit,
    )(masked, value_vectors, spikes, grad_states, keys_part, values_part)
    return grad_queries, grad_keys, grad_values, grad_gate[None], grad_up[None], grad_down[None]


def solution(mesh):
    by_head = P("ctx", "exp")
    by_device = P(("ctx", "exp"), None)
    by_half = P(("ctx", "exp"), None, None)
    return jax.shard_map(
        on_device,
        mesh=mesh,
        in_specs=(by_head,) * 4 + (by_device,) * 2 + (by_half,) * 3 + (by_device,),
        out_specs=(by_head,) * 3 + (by_half,) * 3,
        check_vma=False,
    )
```

time: 424 us -> 368 us (0.87)
  blocking collectives: 248 us -> 155 us
  waiting for transfers between devices: 19.4 us -> 69.9 us
  local copies, waits for them, and re-layouts: 43.8 us -> 7.28 us
  Pallas kernels: 77.8 us -> 93.9 us
  starting transfers between devices: 32.1 us -> 40.4 us
    all_to_all x1 -> x0, blocking collectives: 82.5 us -> none  [on_device(): lax.all_to_all(back_rows.reshape(devices, slots, width), everywhere, 0, 0...]
    all_to_all x3 -> x1, waiting for transfers between devices: 12.7 us -> 60.9 us  [on_device(): lax.all_to_all(back_rows.reshape(devices, slots, width), everywhere, 0, 0...]
    unnamed x73 -> x13, local copies, waits for them, and re-layouts: 41.5 us -> 7.28 us
    all_to_all x2 -> x4, starting transfers between devices: 15.1 us -> 27.2 us  [exchange(): pieces = lax.all_to_all(pieces, 'ctx', 0, 0, tiled=True)]
    all_gather x1 -> x0, blocking collectives: 8.91 us -> none  [on_device(): pack = lax.all_gather(pack, 'exp')]
    all_to_all x3 -> x1, starting transfers between devices: 17.1 us -> 8.38 us  [on_device(): lax.all_to_all(back_rows.reshape(devices, slots, width), everywhere, 0, 0...]
    pallas_call x4 -> x5, Pallas kernels: 41.8 us -> 47.3 us  [the longest x1 23.4 us: on_device(): call(functools.partial(expert_body, exp), (2 * exp,), [pl.BlockSpec((half...]
    ppermute x0 -> x3, starting transfers between devices: none -> 4.88 us  [on_device(): lax.ppermute(pieces[i], 'exp', [(j, (j + i) % exp) for j in range(exp)])]
  transfers between devices with their start and end apart: 5 -> 8, of which waited for: 2 -> 4; matrix products, arithmetic and copies ran while one was open for 1% -> 0% of each run, Pallas kernels for 8% -> 12%
where the time goes in v2:
time: 368 us; the launch traced here: 367 us
  blocking collectives  155 us (42%)
  Pallas kernels  93.9 us (26%)
  waiting for transfers between devices  69.9 us (19%)
  starting transfers between devices  40.4 us (11%)
  local copies, waits for them, and re-layouts  7.28 us (2%)
    all_to_all x1, blocking collectives, on_device(): lax.all_to_all(buffer.reshape(devices, slots, 2 * width), everywhere, 0,...  155 us
    all_to_all x1, waiting for transfers between devices, on_device(): lax.all_to_all(back_rows.reshape(devices, slots, width), everywhere, 0, 0...  60.9 us
    all_to_all x4, starting transfers between devices, exchange(): pieces = lax.all_to_all(pieces, 'ctx', 0, 0, tiled=True)  27.2 us
    pallas_call x1, Pallas kernels, on_device(): call(functools.partial(expert_body, exp), (2 * exp,), [pl.BlockSpec((half...  23.4 us
    pallas_call x1, Pallas kernels, on_device(): call(weights_body, (exp,), [pl.BlockSpec((half_rows, width), lambda i: (i...  14.7 us
    all_to_all x4, waiting for transfers between devices, exchange(): pieces = lax.all_to_all(pieces, 'ctx', 0, 0, tiled=True)  8.98 us
    all_to_all x1, starting transfers between devices, on_device(): lax.all_to_all(back_rows.reshape(devices, slots, width), everywhere, 0, 0...  8.38 us
    pallas_call x1, Pallas kernels, on_device(): call(functools.partial(prepare_body, exp), (1 + pairs,), [smem] + [whole(...  8.31 us
  transfers between devices with their start and end apart: 8, of which 4 were waited for; matrix products, arithmetic and copies ran while one was open for 0% of the time, Pallas kernels for 12%

profile of v2, /device:TPU:1, one launch (start us, length us, event | category | flops | bytes accessed | tf_op | source)
XLA Modules:
  0.0 367.1 jit_solution(17236097429209183496)
XLA Ops:
  0.6 1.4 copy.19.p_ref
  2.0 1.4 copy.18.r_ref
  3.4 1.6 copy.17.s_ref
  5.0 4.5 %shard_map.145 = (bf16[1024,128]{1,0:T(8,128)(2,1)}, bf16[512,1024]{1,0:T(8,128)(2,1)}) custom-call(bf16[512,1024]{1,0:T(8,128)(2,1)} %k_ref.1, bf16[512,1024]{1,0:T(8,128)(2,1)} %v_ref.9, s32[512,8]{1,0:T(8,128)} %copy.17.s_ref), custom_call_target="tpu_custom_call" | custom-call | flops 134217728 | bytes 3145728 | tf_op jit(solution)/shard_map/pallas_call | solution.py:330
  9.5 2.5 shard_map.146
  11.9 9.6 %all-to-all-start = ((bf16[32,32,128]{2,1,0:T(8,128)(2,1)}), bf16[32,32,128]{2,1,0:T(8,128)(2,1)S(1)}, u32[]{:S(2)}, u32[]{:S(2)}) async-start(bf16[32,32,128]{2,1,0:T(8,128)(2,1)} %bitcast.24), calls=%async_computation | async-start | bytes 524288 | tf_op jit(solution)/shard_map/all_to_all | solution.py:321
  21.5 1.3 collective-permute-start
  22.8 2.5 collective-permute-start.1
  25.3 1.2 collective-permute-start.2
  26.4 4.1 %all-to-all-done.x_ref = bf16[32,32,128]{2,1,0:T(8,128)(2,1)S(1)} async-done(((bf16[32,32,128]{2,1,0:T(8,128)(2,1)}), bf16[32,32,128]{2,1,0:T(8,128)(2,1)S(1)}, u32[]{:S(2)}, u32[]{:S(2)}) %all-to-all-start) | async-done | bytes 262176 | tf_op jit(solution)/shard_map/all_to_all | solution.py:321
  30.5 0.9 shard_map.149
  31.4 4.1 %all-to-all-start.1 = ((bf16[32,32,128]{2,1,0:T(8,128)(2,1)}), bf16[32,32,128]{2,1,0:T(8,128)(2,1)S(1)}, u32[]{:S(2)}, u32[]{:S(2)}) async-start(bf16[32,32,128]{2,1,0:T(8,128)(2,1)} %shard_map.149), calls=%async_computation.1 | async-start | bytes 524288 | tf_op jit(solution)/shard_map/all_to_all | solution.py:327
  35.6 5.7 %shard_map.148.intra_ref = f32[512,1024]{1,0:T(8,128)} custom-call(bf16[512,1024]{1,0:T(8,128)(2,1)} %q_ref.7, bf16[512,1024]{1,0:T(8,128)(2,1)} %get-tuple-element.40.mk_ref, bf16[512,1024]{1,0:T(8,128)(2,1)} %v_ref.9), custom_call_target="tpu_custom_call" | custom-call | flops 1073741824 | bytes 5242880 | tf_op jit(solution)/shard_map/pallas_call | solution.py:349
  41.3 0.0 collective-permute-done.refs_1_
  41.3 0.0 copy-start.2
  41.3 0.0 collective-permute-done.1.refs_2_
  41.3 0.0 copy-start.3
  41.3 0.0 collective-permute-done.2.refs_3_
  41.3 0.7 copy-done.2
  42.0 0.1 copy-done.3
  42.1 0.0 copy-start.4
  42.1 0.7 copy-done.4
  42.8 8.3 %shard_map.147 = (bf16[512,1024]{1,0:T(8,128)(2,1)}, bf16[1536,512]{1,0:T(8,128)(2,1)}, bf16[512,1536]{1,0:T(8,128)(2,1)}, bf16[2,2,768,2048]{3,2,1,0:T(8,128)(2,1)}) custom-call(s32[1]{0:T(128)} %bitcast.mine_ref, bf16[144,1024]{1,0:T(8,128)(2,1)} %get-tuple-element.46.refs_0_, bf16[144,1024]{1,0:T(8,128)(2,1)} %copy-done.2, bf16[144,1024]{1,0:T(8,128)(2,1)} %copy-done.3, ...), custom_call_target="tpu_custom_call" | custom-call | flops 1610612736 | bytes 9961472 | tf_op jit(solution)/shard_map/pallas_call | solution.py:357
  51.2 0.0 all-to-all-done.1
  51.2 0.0 copy-start
  51.2 0.7 copy-done
  51.9 7.1 %shard_map.150 = bf16[2,2,768,2048]{3,2,1,0:T(8,128)(2,1)} custom-call(bf16[1536,512]{1,0:T(8,128)(2,1)} %get-tuple-element.51.m_ref, bf16[512,1024]{1,0:T(8,128)(2,1)} %q_ref.7, f32[512,1024]{1,0:T(8,128)} %shard_map.148.intra_ref, bf16[1024,128]{1,0:T(8,128)(2,1)} %bitcast.21, ...), custom_call_target="tpu_custom_call", output_to_operand_aliasing={{}: (4, {})} | custom-call | flops 1610612736 | bytes 9961472 | tf_op jit(solution)/shard_map/pallas_call | solution.py:368
  59.0 154.8 %all_to_all.30 = bf16[128,24,2048]{2,1,0:T(8,128)(2,1)} all-to-all(bf16[128,24,2048]{2,1,0:T(8,128)(2,1)} %bitcast.19), channel_id=1, replica_groups=mesh['ctx'=32,'exp'=4] {'exp','ctx'}, dimensions={0} | all-to-all | bytes 25165824 | tf_op jit(solution)/shard_map/all_to_all | solution.py:374
  213.8 23.4 %shard_map.151 = (bf16[3072,1024]{1,0:T(8,128)(2,1)}, bf16[768,384]{1,0:T(8,128)(2,1)}, bf16[768,768]{1,0:T(8,128)(2,1)}) custom-call(bf16[3072,2048]{1,0:T(8,128)(2,1)} %bitcast.15, bf16[3072,2048]{1,0:T(8,128)(2,1)} %bitcast.16, bf16[4096,384]{1,0:T(8,128)(2,1)} %bitcast.26, bf16[4096,384]{1,0:T(8,128)(2,1)} %bitcast.27, bf16[384,4096]{1,0:T(8,128)(2,1)} %bitcast.28), custom_call_target="tpu_custom_call" | custom-call | flops 12079595520 | bytes 34603008 | tf_op jit(solution)/shard_map/pallas_call | solution.py:381
  237.2 8.4 %all-to-all-start.3 = ((bf16[128,24,1024]{2,1,0:T(8,128)(2,1)}), bf16[128,24,1024]{2,1,0:T(8,128)(2,1)}, u32[]{:S(2)}, u32[]{:S(2)}) async-start(bf16[128,24,1024]{2,1,0:T(8,128)(2,1)} %bitcast.20), calls=%async_computation.3 | async-start | bytes 12582912 | tf_op jit(solution)/shard_map/all_to_all | solution.py:399
  245.6 14.7 %shard_map.152 = (bf16[4096,384]{1,0:T(8,128)(2,1)}, bf16[4096,384]{1,0:T(8,128)(2,1)}, bf16[384,4096]{1,0:T(8,128)(2,1)}) custom-call(bf16[3072,2048]{1,0:T(8,128)(2,1)} %bitcast.17, bf16[3072,2048]{1,0:T(8,128)(2,1)} %bitcast.18, bf16[768,384]{1,0:T(8,128)(2,1)} %get-tuple-element.55.h_ref, bf16[768,768]{1,0:T(8,128)(2,1)} %get-tuple-element.56.a_ref), custom_call_target="tpu_custom_call" | custom-call | flops 7247757312 | bytes 22020096 | tf_op jit(solution)/shard_map/pallas_call | solution.py:402
  260.3 60.9 %all-to-all-done.3 = bf16[128,24,1024]{2,1,0:T(8,128)(2,1)} async-done(((bf16[128,24,1024]{2,1,0:T(8,128)(2,1)}), bf16[128,24,1024]{2,1,0:T(8,128)(2,1)}, u32[]{:S(2)}, u32[]{:S(2)}) %all-to-all-start.3) | async-done | bytes 6291488 | tf_op jit(solution)/shard_map/all_to_all | solution.py:399
  321.2 7.2 %shard_map.153 = (bf16[512,1024]{1,0:T(8,128)(2,1)}, bf16[1024,128]{1,0:T(8,128)(2,1)}) custom-call(bf16[512,1536]{1,0:T(8,128)(2,1)} %get-tuple-element.50.mt_ref, bf16[4,768,1024]{2,1,0:T(8,128)(2,1)} %bitcast.9.ret_ref, bf16[512,1024]{1,0:T(8,128)(2,1)} %get-tuple-element.61.og_ref, bf16[512,1024]{1,0:T(8,128)(2,1)} %q_ref.7), custom_call_target="tpu_custom_call" | custom-call | flops 1610612736 | bytes 11010048 | tf_op jit(solution)/shard_map/pallas_call | solution.py:423
  328.4 7.5 %all-to-all-start.4 = ((bf16[32,32,128]{2,1,0:T(8,128)(2,1)}), bf16[32,32,128]{2,1,0:T(8,128)(2,1)S(1)}, u32[]{:S(2)}, u32[]{:S(2)}) async-start(bf16[32,32,128]{2,1,0:T(8,128)(2,1)} %bitcast.25), calls=%async_computation.4 | async-start | bytes 524288 | tf_op jit(solution)/shard_map/all_to_all | solution.py:321
  335.9 7.6 %shard_map.155 = (f32[512,1024]{1,0:T(8,128)}, f32[512,1024]{1,0:T(8,128)}) custom-call(bf16[512,1024]{1,0:T(8,128)(2,1)} %q_ref.7, bf16[512,1024]{1,0:T(8,128)(2,1)} %get-tuple-element.40.mk_ref, bf16[512,1024]{1,0:T(8,128)(2,1)} %v_ref.9, bf16[512,1024]{1,0:T(8,128)(2,1)} %get-tuple-element.62.ag_ref), custom_call_target="tpu_custom_call" | custom-call | flops 2147483648 | bytes 8388608 | tf_op jit(solution)/shard_map/pallas_call | solution.py:429
  343.5 1.4 all-to-all-done.4.x_ref
  344.9 0.9 shard_map.156
  345.7 6.0 %all-to-all-start.5 = ((bf16[32,32,128]{2,1,0:T(8,128)(2,1)}), bf16[32,32,128]{2,1,0:T(8,128)(2,1)S(1)}, u32[]{:S(2)}, u32[]{:S(2)}) async-start(bf16[32,32,128]{2,1,0:T(8,128)(2,1)} %shard_map.156), calls=%async_computation.5 | async-start | bytes 524288 | tf_op jit(solution)/shard_map/all_to_all | solution.py:327
  351.7 5.5 %shard_map.154 = bf16[512,1024]{1,0:T(8,128)(2,1)} custom-call(bf16[512,1024]{1,0:T(8,128)(2,1)} %get-tuple-element.40.mk_ref, bf16[512,1024]{1,0:T(8,128)(2,1)} %v_ref.9, bf16[512,1024]{1,0:T(8,128)(2,1)} %get-tuple-element.62.ag_ref, bf16[1024,128]{1,0:T(8,128)(2,1)} %bitcast.22), custom_call_target="tpu_custom_call" | custom-call | flops 1073741824 | bytes 4194304 | tf_op jit(solution)/shard_map/pallas_call | solution.py:434
  357.2 3.5 all-to-all-done.5
  360.7 0.0 copy-start.1
  360.7 0.7 copy-done.1
  361.4 5.6 %shard_map.157 = (bf16[512,1024]{1,0:T(8,128)(2,1)}, bf16[512,1024]{1,0:T(8,128)(2,1)}) custom-call(bf16[512,1024]{1,0:T(8,128)(2,1)} %get-tuple-element.40.mk_ref, bf16[512,1024]{1,0:T(8,128)(2,1)} %v_ref.9, s32[512,8]{1,0:T(8,128)} %copy.17.s_ref, bf16[1024,128]{1,0:T(8,128)(2,1)} %bitcast.23, f32[512,1024]{1,0:T(8,128)} %get-tuple-element.67.gki_ref, ...), custom_call_target="tpu_custom_call" | custom-call | flops 268435456 | bytes 8388608 | tf_op jit(solution)/shard_map/pallas_call | solution.py:438
Async XLA Ops:
  11.9 18.6 %all-to-all-start = ((bf16[32,32,128]{2,1,0:T(8,128)(2,1)}), bf16[32,32,128]{2,1,0:T(8,128)(2,1)S(1)}, u32[]{:S(2)}, u32[]{:S(2)}) async-start(bf16[32,32,128]{2,1,0:T(8,128)(2,1)} %bitcast.24), calls=%async_computation | async-start | bytes 524288 | tf_op jit(solution)/shard_map/all_to_all | solution.py:321
  21.5 19.8 %collective-permute-start = (bf16[144,1024]{1,0:T(8,128)(2,1)}, bf16[144,1024]{1,0:T(8,128)(2,1)S(1)}, u32[]{:S(2)}, u32[]{:S(2)}) collective-permute-start(bf16[144,1024]{1,0:T(8,128)(2,1)} %get-tuple-element.47), channel_id=1, source_target_pairs={{0,1},{1,2},{2,3},{3,0},{4,5},{5,6},{6,7},{7,4},{8,9},{9,10},{10,1... | collective-permute-start | bytes 884744 | tf_op jit(solution)/shard_map/ppermute | solution.py:345
  22.8 18.5 %collective-permute-start.1 = (bf16[144,1024]{1,0:T(8,128)(2,1)}, bf16[144,1024]{1,0:T(8,128)(2,1)S(1)}, u32[]{:S(2)}, u32[]{:S(2)}) collective-permute-start(bf16[144,1024]{1,0:T(8,128)(2,1)} %get-tuple-element.48), channel_id=1, source_target_pairs={{0,2},{1,3},{2,0},{3,1},{4,6},{5,7},{6,4},{7,5},{8,10},{9,11},{10,... | collective-permute-start | bytes 884744 | tf_op jit(solution)/shard_map/ppermute | solution.py:345
  25.3 16.1 %collective-permute-start.2 = (bf16[144,1024]{1,0:T(8,128)(2,1)}, bf16[144,1024]{1,0:T(8,128)(2,1)S(1)}, u32[]{:S(2)}, u32[]{:S(2)}) collective-permute-start(bf16[144,1024]{1,0:T(8,128)(2,1)} %get-tuple-element.49), channel_id=1, source_target_pairs={{0,3},{1,0},{2,1},{3,2},{4,7},{5,4},{6,5},{7,6},{8,11},{9,8},{10,9... | collective-permute-start | bytes 884744 | tf_op jit(solution)/shard_map/ppermute | solution.py:345
  31.4 19.7 %all-to-all-start.1 = ((bf16[32,32,128]{2,1,0:T(8,128)(2,1)}), bf16[32,32,128]{2,1,0:T(8,128)(2,1)S(1)}, u32[]{:S(2)}, u32[]{:S(2)}) async-start(bf16[32,32,128]{2,1,0:T(8,128)(2,1)} %shard_map.149), calls=%async_computation.1 | async-start | bytes 524288 | tf_op jit(solution)/shard_map/all_to_all | solution.py:327
  41.3 0.7 copy-start.2
  41.3 0.8 copy-start.3
  42.1 0.7 copy-start.4
  51.2 0.7 copy-start
  237.2 84.0 %all-to-all-start.3 = ((bf16[128,24,1024]{2,1,0:T(8,128)(2,1)}), bf16[128,24,1024]{2,1,0:T(8,128)(2,1)}, u32[]{:S(2)}, u32[]{:S(2)}) async-start(bf16[128,24,1024]{2,1,0:T(8,128)(2,1)} %bitcast.20), calls=%async_computation.3 | async-start | bytes 12582912 | tf_op jit(solution)/shard_map/all_to_all | solution.py:399
  328.4 16.5 %all-to-all-start.4 = ((bf16[32,32,128]{2,1,0:T(8,128)(2,1)}), bf16[32,32,128]{2,1,0:T(8,128)(2,1)S(1)}, u32[]{:S(2)}, u32[]{:S(2)}) async-start(bf16[32,32,128]{2,1,0:T(8,128)(2,1)} %bitcast.25), calls=%async_computation.4 | async-start | bytes 524288 | tf_op jit(solution)/shard_map/all_to_all | solution.py:321
  345.7 15.0 %all-to-all-start.5 = ((bf16[32,32,128]{2,1,0:T(8,128)(2,1)}), bf16[32,32,128]{2,1,0:T(8,128)(2,1)S(1)}, u32[]{:S(2)}, u32[]{:S(2)}) async-start(bf16[32,32,128]{2,1,0:T(8,128)(2,1)} %shard_map.156), calls=%async_computation.5 | async-start | bytes 524288 | tf_op jit(solution)/shard_map/all_to_all | solution.py:327
  360.7 0.7 copy-start.1

commit v3 on v2

--- a/solution.py
+++ b/solution.py
@@ -37,11 +37,11 @@
 
 
 def spike_columns(spikes, pair, width, head):
-    heads = spikes.shape[1]
+    heads = spikes.shape[0]
     col = lax.broadcasted_iota(jnp.int32, (heads, width), 1) // head + pair * (width // head)
     row = lax.broadcasted_iota(jnp.int32, (heads, width), 0)
     spread = jnp.where(col == row, 1.0, 0.0).astype(BF16)
-    return mm(spikes.astype(F32).astype(BF16), spread)
+    return mm(spikes.astype(F32).astype(BF16), spread, TN)
 
 
 def cut_body(capacity, slots, half_rows, mine_ref, x_ref, r_ref, p_ref, *o_refs):
@@ -51,24 +51,24 @@
     row = lax.broadcasted_iota(jnp.int32, (tokens, tokens), 0)
     col = lax.broadcasted_iota(jnp.int32, (tokens, tokens), 1)
 
-    def lanes(column):
-        return jnp.sum(jnp.where(row == col, column, 0.0), axis=0, keepdims=True)
+    def column(lanes):
+        return jnp.sum(jnp.where(row == col, lanes, 0.0), axis=1, keepdims=True)
 
     named = r_ref[...].astype(F32)
     probs = p_ref[...].astype(F32)
     line = lax.broadcasted_iota(jnp.int32, (extra, tokens), 0)
     pack = jnp.zeros((extra, tokens), F32)
+    first, second = column(named[0:1, :]), column(named[1:2, :])
     for k in range(2):
-        expert = lanes(named[:, k : k + 1])
-        same = jnp.where(named[:, 0:1] == expert, 1.0, 0.0)
-        same = same + jnp.where(named[:, 1:2] == expert, 1.0, 0.0)
+        expert = named[k : k + 1, :]
+        same = jnp.where(first == expert, 1.0, 0.0) + jnp.where(second == expert, 1.0, 0.0)
         slot = jnp.sum(jnp.where(row < col, same, 0.0), axis=0, keepdims=True)
         half = jnp.floor(expert * 0.5)
         place = (expert - 2.0 * half) * half_rows + half * slots + slot
         place = place + (mine_ref[0] * capacity).astype(F32)
         high = jnp.floor(place * 0.125)
         for at, value in (
-            (3 * k, high), (3 * k + 1, place - 8.0 * high), (3 * k + 2, lanes(probs[:, k : k + 1]))
+            (3 * k, high), (3 * k + 1, place - 8.0 * high), (3 * k + 2, probs[k : k + 1, :])
         ):
             pack = jnp.where(line == at, value, pack)
     for i, o_ref in enumerate(o_refs):
@@ -79,7 +79,7 @@
 
 
 def prepare_body(count, mine_ref, *refs):
-    x_refs, (g_ref, m_ref, mt_ref, o_ref, w_ref) = refs[:count], refs[count:]
+    x_refs, (g_ref, m_ref, o_ref, w_ref) = refs[:count], refs[count:]
     rows = m_ref.shape[0]
     tokens = g_ref.shape[0] // count
     pair = o_ref.shape[3]
@@ -88,10 +88,6 @@
     @pl.when(step == 0)
     def _():
         down = lax.broadcasted_iota(jnp.int32, (rows, tokens), 0).astype(F32)
-        across = lax.broadcasted_iota(jnp.int32, (tokens, rows), 1).astype(F32)
-        eye = lax.broadcasted_iota(jnp.int32, (tokens, tokens), 0) == lax.broadcasted_iota(
-            jnp.int32, (tokens, tokens), 1
-        )
         for i, x_ref in enumerate(x_refs):
             at = pl.multiple_of(lax.rem(mine_ref[0] + count - i, count) * tokens, tokens)
             g_ref[pl.ds(at, tokens), :] = x_ref[:tokens, :]
@@ -103,11 +99,6 @@
             w_ref[:, pl.ds(at, tokens)] = jnp.where(
                 hit0, pack[2:3], jnp.where(hit1, pack[5:6], 0.0)
             ).astype(BF16)
-            first = jnp.sum(jnp.where(eye, first, 0.0), axis=1, keepdims=True)
-            second = jnp.sum(jnp.where(eye, second, 0.0), axis=1, keepdims=True)
-            mt_ref[pl.ds(at, tokens), :] = jnp.where(
-                (across == first) | (across == second), 1.0, 0.0
-            ).astype(BF16)
 
     @pl.when(step > 0)
     def _():
@@ -126,17 +117,6 @@
         bs_ref[cols, :] = mm(masked[:, cols], value[:, cols], TN).astype(BF16)
 
 
-def intra_body(head, q_ref, mk_ref, v_ref, o_ref):
-    length, width = q_ref.shape
-    t = lax.broadcasted_iota(jnp.int32, (length, length), 0)
-    s = lax.broadcasted_iota(jnp.int32, (length, length), 1)
-    for h in range(width // head):
-        cols = slice(h * head, (h + 1) * head)
-        scores = mm(q_ref[:, cols], mk_ref[:, cols], NT)
-        scores = jnp.where(t >= s, scores, 0.0).astype(BF16)
-        o_ref[:, cols] = mm(scores, v_ref[:, cols])
-
-
 def sum_body(reverse, x_ref, o_ref):
     count = x_ref.shape[0]
 
@@ -146,6 +126,25 @@
         return total + x_ref[at].astype(F32)
 
     lax.fori_loop(0, count, step, jnp.zeros(x_ref.shape[1:], F32))
+
+
+def select_t_body(count, mine_ref, *refs):
+    x_refs, mt_ref = refs[:count], refs[count]
+    rows = mt_ref.shape[1]
+    tokens = mt_ref.shape[0] // count
+    across = lax.broadcasted_iota(jnp.int32, (tokens, rows), 1).astype(F32)
+    eye = lax.broadcasted_iota(jnp.int32, (tokens, tokens), 0) == lax.broadcasted_iota(
+        jnp.int32, (tokens, tokens), 1
+    )
+    for i, x_ref in enumerate(x_refs):
+        at = pl.multiple_of(lax.rem(mine_ref[0] + count - i, count) * tokens, tokens)
+        pack = x_ref[tokens:, :tokens].astype(F32)
+        first, second = 8.0 * pack[0:1] + pack[1:2], 8.0 * pack[3:4] + pack[4:5]
+        first = jnp.sum(jnp.where(eye, first, 0.0), axis=1, keepdims=True)
+        second = jnp.sum(jnp.where(eye, second, 0.0), axis=1, keepdims=True)
+        mt_ref[pl.ds(at, tokens), :] = jnp.where(
+            (across == first) | (across == second), 1.0, 0.0
+        ).astype(BF16)
 
 
 def put_rows(m_ref, columns, o_ref):
@@ -156,53 +155,60 @@
         o_ref[p, 1] = picked
 
 
-def rows_body(head, scaling, m_ref, q_ref, intra_ref, s_ref, buf_ref, o_ref):
+def rows_body(head, scaling, m_ref, q_ref, mk_ref, v_ref, s_ref, buf_ref, o_ref):
     del buf_ref
-    width = q_ref.shape[1]
+    length, width = q_ref.shape
+    t = lax.broadcasted_iota(jnp.int32, (length, length), 0)
+    s = lax.broadcasted_iota(jnp.int32, (length, length), 1)
     parts = []
     for h in range(width // head):
         cols = slice(h * head, (h + 1) * head)
-        inter = mm(q_ref[:, cols], s_ref[cols, :])
-        parts.append((scaling * (intra_ref[:, cols] + inter)).astype(BF16))
+        scores = mm(q_ref[:, cols], mk_ref[:, cols], NT)
+        scores = jnp.where(t >= s, scores, 0.0).astype(BF16)
+        total = mm(scores, v_ref[:, cols]) + mm(q_ref[:, cols], s_ref[cols, :])
+        parts.append((scaling * total).astype(BF16))
     put_rows(m_ref, jnp.concatenate(parts, axis=1), o_ref)
 
 
 def expert_body(
-    steps, r_ref, g_ref, wg_ref, wu_ref, wd_ref, ret_ref, h_ref, a_ref, gate, up, hid
+    steps, r_ref, g_ref, wg_ref, wu_ref, wd_ref, ret_ref, h_ref, a_ref, both, hid, cat
 ):
     i = pl.program_id(0)
-    rows, width = hid.shape
+    rows, hidden = hid.shape
+    width = r_ref.shape[1]
     chunk = rows // 6
+    part = pl.ds(pl.multiple_of(lax.rem(i, steps) * width, width), width)
+
+    @pl.when(i < steps)
+    def _():
+        cat[part, :hidden] = wg_ref[...]
+        cat[part, hidden:] = wu_ref[...]
 
     @pl.when(i == 0)
     def _():
-        gate[...] = mm(r_ref[...], wg_ref[...])
-        up[...] = mm(r_ref[...], wu_ref[...])
+        both[...] = mm(r_ref[...], cat[part, :])
         hid[...] = mm(g_ref[...], wd_ref[...], NT)
 
     @pl.when((i > 0) & (i < steps))
     def _():
-        gate[...] += mm(r_ref[...], wg_ref[...])
-        up[...] += mm(r_ref[...], wu_ref[...])
+        both[...] += mm(r_ref[...], cat[part, :])
         hid[...] += mm(g_ref[...], wd_ref[...], NT)
 
     @pl.when(i == steps - 1)
     def _():
         @pl.loop(0, rows // chunk)
         def _(c):
-            part = pl.ds(pl.multiple_of(c * chunk, chunk), chunk)
-            g, u, d = gate[part, :], up[part, :], hid[part, :]
+            at = pl.ds(pl.multiple_of(c * chunk, chunk), chunk)
+            g, u, d = both[at, :hidden], both[at, hidden:], hid[at, :]
             sig = jax.nn.sigmoid(g)
             silu = g * sig
-            h_ref[part, :] = (silu * u).astype(BF16)
-            a_ref[part, :width] = (d * u * (sig * (1.0 + g * (1.0 - sig)))).astype(BF16)
-            a_ref[part, width:] = (d * silu).astype(BF16)
+            h_ref[at, :] = (silu * u).astype(BF16)
+            a_ref[at, :hidden] = (d * u * (sig * (1.0 + g * (1.0 - sig)))).astype(BF16)
+            a_ref[at, hidden:] = (d * silu).astype(BF16)
 
     @pl.when(i >= steps)
     def _():
-        ret_ref[...] = (
-            mm(a_ref[:, :width], wg_ref[...], NT) + mm(a_ref[:, width:], wu_ref[...], NT)
-        ).astype(BF16)
+        ret_ref[...] = mm(a_ref[...], cat[part, :], NT).astype(BF16)
 
 
 def weights_body(r_ref, g_ref, h_ref, a_ref, dg_ref, du_ref, dd_ref):
@@ -300,7 +306,7 @@
     slots = exp * capacity
     half_rows = ctx * slots
     rows = 2 * half_rows
-    pair = 2 * head
+    pair = 4 * head
     pairs = width // pair
     everywhere = ("exp", "ctx")
 
@@ -315,6 +321,7 @@
     seq = shape(length, width)
     seq32 = shape(length, width, dtype=F32)
     unit = length * width * 2
+    spikes_t = spikes.T
 
     def exchange(part, reverse, cover):
         pieces = part.reshape(ctx, heads * head // ctx, head)
@@ -329,48 +336,43 @@
 
     block_state, masked = call(
         functools.partial(state_body, head), (pairs,),
-        [wide, wide, whole(length, heads)], [tall, wide],
+        [wide, wide, whole(heads, length)], [tall, wide],
         [shape(heads * head, head), seq], 2 * length * width * head, 3 * unit,
-    )(key_vectors, value_vectors, spikes)
+    )(key_vectors, value_vectors, spikes_t)
     mine = lax.axis_index("exp").reshape(1)
     smem = pl.BlockSpec(memory_space=pltpu.SMEM)
     piece = (tokens + 16, width)
+    own_grad, block_state = lax.optimization_barrier((out_grad, block_state))
     pieces = call(
         functools.partial(cut_body, capacity, slots, half_rows), (1,),
-        [smem, whole(tokens, model), whole(tokens, top), whole(tokens, top)],
+        [smem, whole(tokens, model), whole(top, tokens), whole(top, tokens)],
         [whole(*piece)] * exp, [shape(*piece)] * exp, 1e6, 2 * unit,
-    )(mine, out_grad, routes, route_probs)
-    pieces, block_state = lax.optimization_barrier((tuple(pieces), block_state))
+    )(mine, own_grad, routes.T, route_probs.T)
     pieces = [pieces[0]] + [
         lax.ppermute(pieces[i], "exp", [(j, (j + i) % exp) for j in range(exp)])
         for i in range(1, exp)
     ]
     states_in, _ = exchange(block_state, False, ())
-    intra = call(
-        functools.partial(intra_body, head), (pairs,), [wide] * 3, wide, seq32,
-        4 * length * length * width, 5 * unit,
-    )(queries, masked, value_vectors)
-
     send_shape = shape(2, 2, half_rows, 2 * width)
     send_flops = 2 * rows * length * width
     send_bytes = 4 * rows * width + 2 * rows * length + 2 * unit
-    grad_cols, select, select_t, buffer = call(
+    grad_cols, select, buffer = call(
         functools.partial(prepare_body, exp), (1 + pairs,), [smem] + [whole(*piece)] * exp,
         [
-            whole(length, width), whole(rows, length), whole(length, rows),
+            whole(length, width), whole(rows, length),
             pl.BlockSpec(
                 (2, 2, half_rows, pair), lambda i: (0, 0, 0, jnp.maximum(i - 1, 0) + pairs)
             ),
         ],
-        [seq, shape(rows, length), shape(length, rows), send_shape], send_flops, send_bytes,
+        [seq, shape(rows, length), send_shape], send_flops, send_bytes,
         scratch_shapes=[pltpu.VMEM((rows, length), BF16)],
     )(mine, *pieces)
     buffer = call(
         functools.partial(rows_body, head, scaling), (pairs,),
-        [whole(rows, length), wide, wide, tall, pl.BlockSpec(memory_space=pl.ANY)],
+        [whole(rows, length), wide, wide, wide, tall, pl.BlockSpec(memory_space=pl.ANY)],
         pl.BlockSpec((2, 2, half_rows, pair), lambda i: (0, 0, 0, i)),
-        send_shape, send_flops, send_bytes, input_output_aliases={4: 0},
-    )(select, queries, intra, states_in, buffer)
+        send_shape, send_flops, send_bytes, 52, input_output_aliases={5: 0},
+    )(select, queries, masked, value_vectors, states_in, buffer)
     got = lax.all_to_all(
         buffer.reshape(devices, slots, 2 * width), everywhere, 0, 0, tiled=True
     ).reshape(exp * half_rows, 2 * width)
@@ -383,8 +385,8 @@
         [
             pl.BlockSpec((half_rows, width), lambda i: (jnp.minimum(i, last), 0)),
             pl.BlockSpec((half_rows, width), lambda i: (jnp.minimum(i, last), 1)),
-            pl.BlockSpec((width, hidden), lambda i: (i % exp, 0)),
-            pl.BlockSpec((width, hidden), lambda i: (i % exp, 0)),
+            pl.BlockSpec((width, hidden), lambda i: (jnp.minimum(i, last), 0)),
+            pl.BlockSpec((width, hidden), lambda i: (jnp.minimum(i, last), 0)),
             pl.BlockSpec((hidden, width), lambda i: (0, jnp.minimum(i, last))),
         ],
         [
@@ -394,7 +396,10 @@
         ],
         [shape(exp * half_rows, width), act, shape(half_rows, 2 * hidden)],
         10 * half_rows * model * hidden, 12 * block + 10 * model * hidden,
-        scratch_shapes=[pltpu.VMEM((half_rows, hidden), F32)] * 3,
+        scratch_shapes=[
+            pltpu.VMEM((half_rows, 2 * hidden), F32), pltpu.VMEM((half_rows, hidden), F32),
+            pltpu.VMEM((model, 2 * hidden), BF16),
+        ],
     )(got, got, gate_weight[0], up_weight[0], down_weight[0])
     returned = lax.all_to_all(
         back_rows.reshape(devices, slots, width), everywhere, 0, 0, tiled=True
@@ -416,8 +421,13 @@
         6 * half_rows * model * hidden, 8 * block + 6 * model * hidden,
     )(got, got, hid, acts)
 
-    returned, grad_gate, grad_up, grad_down = lax.optimization_barrier(
-        (returned, grad_gate, grad_up, grad_down)
+    far_pieces, acts = lax.optimization_barrier((tuple(pieces), acts))
+    select_t = call(
+        functools.partial(select_t_body, exp), (1,), [smem] + [whole(*piece)] * exp,
+        whole(length, rows), shape(length, rows), 1e6, 2 * rows * length + unit,
+    )(mine, *far_pieces)
+    returned, select_t, grad_gate, grad_up, grad_down = lax.optimization_barrier(
+        (returned, select_t, grad_gate, grad_up, grad_down)
     )
 
     att_grad, local_grad = call(
@@ -437,9 +447,9 @@
     )(masked, value_vectors, att_grad, states_in)
     grad_keys, grad_values = call(
         functools.partial(final_body, head), (pairs,),
-        [wide, wide, whole(length, heads), tall, wide, wide], [wide] * 2, [seq, seq],
-        4 * length * width * head, 8 * unit,
-    )(masked, value_vectors, spikes, grad_states, keys_part, values_part)
+        [wide, wide, whole(heads, length), tall, wide, wide], [wide] * 2, [seq, seq],
+        4 * length * width * head, 8 * unit, 52,
+    )(masked, value_vectors, spikes_t, grad_states, keys_part, values_part)
     return grad_queries, grad_keys, grad_values, grad_gate[None], grad_up[None], grad_down[None]
 
 

time: 368 us -> 351 us (0.954)
  Pallas kernels: 93.9 us -> 83.3 us
  local copies, waits for them, and re-layouts: 7.28 us -> 0.81 us
    unnamed x13 -> x14, local copies, waits for them, and re-layouts: 7.28 us -> 0.81 us
    pallas_call x3, Pallas kernels: 15.9 us -> 10.3 us  [the longest x1 4.18 us: on_device(): call(functools.partial(final_body, head), (pairs,), [wide, wide, whole(he...]
  transfers between devices with their start and end apart: 8 -> 8, of which waited for: 4 -> 5; matrix products, arithmetic and copies ran while one was open for 0% -> 0% of each run, Pallas kernels for 12% -> 11%
where the time goes in v3:
time: 351 us
  blocking collectives  155 us (44%)
  Pallas kernels  83.3 us (24%)
  waiting for transfers between devices  68.1 us (19%)
  starting transfers between devices  42.2 us (12%)
    all_to_all x1, blocking collectives, on_device(): lax.all_to_all(buffer.reshape(devices, slots, 2 * width), everywhere, 0,...  155 us
    all_to_all x1, waiting for transfers between devices, on_device(): lax.all_to_all(back_rows.reshape(devices, slots, width), everywhere, 0, 0...  58 us
    all_to_all x4, starting transfers between devices, exchange(): pieces = lax.all_to_all(pieces, 'ctx', 0, 0, tiled=True)  29.7 us
    pallas_call x1, Pallas kernels, on_device(): call(functools.partial(expert_body, exp), (2 * exp,), [pl.BlockSpec((half...  20.7 us
    pallas_call x1, Pallas kernels, on_device(): call(weights_body, (exp,), [pl.BlockSpec((half_rows, width), lambda i: (i...  14.6 us
    pallas_call x1, Pallas kernels, on_device(): call(functools.partial(rows_body, head, scaling), (pairs,), [whole(rows,...  8.18 us
    all_to_all x1, starting transfers between devices, on_device(): lax.all_to_all(back_rows.reshape(devices, slots, width), everywhere, 0, 0...  7.73 us
    pallas_call x1, Pallas kernels, on_device(): call(functools.partial(back_body, head, scaling), (pairs,), [wide] * 4, [...  7.59 us
  transfers between devices with their start and end apart: 8, of which 5 were waited for; matrix products, arithmetic and copies ran while one was open for 0% of the time, Pallas kernels for 11%

profile of v3, /device:TPU:1, one launch (start us, length us, event | category | flops | bytes accessed | tf_op | source)
XLA Modules:
  0.0 350.6 jit_solution(672027838012955002)
XLA Ops:
  0.6 3.2 shard_map.145
  3.8 9.6 %all-to-all-start = ((bf16[32,32,128]{2,1,0:T(8,128)(2,1)}), bf16[32,32,128]{2,1,0:T(8,128)(2,1)S(1)}, u32[]{:S(2)}, u32[]{:S(2)}) async-start(bf16[32,32,128]{2,1,0:T(8,128)(2,1)} %bitcast.29), calls=%async_computation | async-start | bytes 524288 | tf_op jit(solution)/shard_map/all_to_all | solution.py:328
  13.4 2.4 shard_map.146
  15.8 1.2 collective-permute-start
  17.0 2.5 collective-permute-start.1
  19.5 1.2 collective-permute-start.2
  20.6 1.8 all-to-all-done.x_ref
  22.4 0.9 shard_map.148
  23.3 0.0 copy-start.1
  23.3 6.6 %all-to-all-start.1 = ((bf16[32,32,128]{2,1,0:T(8,128)(2,1)}), bf16[32,32,128]{2,1,0:T(8,128)(2,1)S(1)}, u32[]{:S(2)}, u32[]{:S(2)}) async-start(bf16[32,32,128]{2,1,0:T(8,128)(2,1)} %shard_map.148), calls=%async_computation.1 | async-start | bytes 524288 | tf_op jit(solution)/shard_map/all_to_all | solution.py:334
  29.9 0.0 collective-permute-done.refs_1_
  29.9 0.0 copy-start.4
  29.9 3.0 collective-permute-done.1.refs_2_
  32.9 0.0 copy-start.5
  32.9 0.0 collective-permute-done.2.refs_3_
  32.9 0.0 copy-start.6
  32.9 0.0 copy-done.4
  32.9 0.7 copy-done.5
  33.6 0.1 copy-done.6
  33.7 6.7 %shard_map.147 = (bf16[512,1024]{1,0:T(8,128)(2,1)}, bf16[1536,512]{1,0:T(8,128)(2,1)}, bf16[2,2,768,2048]{3,2,1,0:T(8,128)(2,1)}) custom-call(s32[1]{0:T(128)} %bitcast.1.mine_ref, bf16[144,1024]{1,0:T(8,128)(2,1)} %get-tuple-element.53.refs_0_, bf16[144,1024]{1,0:T(8,128)(2,1)} %copy-done.4, bf16[144,1024]{1,0:T(8,128)(2,1)} %copy-done.5, ...), custom_call_target="tpu_custom_call" | custom-call | flops 1610612736 | bytes 9961472 | tf_op jit(solution)/shard_map/pallas_call | solution.py:359
  40.4 0.0 all-to-all-done.1
  40.4 0.0 copy-start.2
  40.4 0.0 copy-done.1
  40.4 8.2 %shard_map.149 = bf16[2,2,768,2048]{3,2,1,0:T(8,128)(2,1)} custom-call(bf16[1536,512]{1,0:T(8,128)(2,1)} %get-tuple-element.48.m_ref, bf16[512,1024]{1,0:T(8,128)(2,1)S(1)} %copy-done.1, bf16[512,1024]{1,0:T(8,128)(2,1)} %get-tuple-element.41.mk_ref, bf16[512,1024]{1,0:T(8,128)(2,1)} %v_ref.9, ...), custom_call_target="tpu_custom_call", output_to_operand_aliasing={{}: (5, {})} | custom-call | flops 1610612736 | bytes 9961472 | tf_op jit(solution)/shard_map/pallas_call | solution.py:370
  48.6 0.0 copy-done.2
  48.6 155.4 %all_to_all.30 = bf16[128,24,2048]{2,1,0:T(8,128)(2,1)} all-to-all(bf16[128,24,2048]{2,1,0:T(8,128)(2,1)} %bitcast.27), channel_id=1, replica_groups=mesh['ctx'=32,'exp'=4] {'exp','ctx'}, dimensions={0} | all-to-all | bytes 25165824 | tf_op jit(solution)/shard_map/all_to_all | solution.py:376
  204.0 20.7 %shard_map.150 = (bf16[3072,1024]{1,0:T(8,128)(2,1)}, bf16[768,384]{1,0:T(8,128)(2,1)}, bf16[768,768]{1,0:T(8,128)(2,1)}) custom-call(bf16[3072,2048]{1,0:T(8,128)(2,1)} %bitcast.23, bf16[3072,2048]{1,0:T(8,128)(2,1)} %bitcast.24, bf16[4096,384]{1,0:T(8,128)(2,1)} %bitcast.33, bf16[4096,384]{1,0:T(8,128)(2,1)} %bitcast.34, bf16[384,4096]{1,0:T(8,128)(2,1)} %bitcast.35), custom_call_target="tpu_custom_call" | custom-call | flops 12079595520 | bytes 34603008 | tf_op jit(solution)/shard_map/pallas_call | solution.py:383
  224.7 7.7 %all-to-all-start.3 = ((bf16[128,24,1024]{2,1,0:T(8,128)(2,1)}), bf16[128,24,1024]{2,1,0:T(8,128)(2,1)}, u32[]{:S(2)}, u32[]{:S(2)}) async-start(bf16[128,24,1024]{2,1,0:T(8,128)(2,1)} %bitcast.28), calls=%async_computation.3 | async-start | bytes 12582912 | tf_op jit(solution)/shard_map/all_to_all | solution.py:404
  232.5 2.9 shard_map.151.mt_ref
  235.4 14.6 %shard_map.152 = (bf16[4096,384]{1,0:T(8,128)(2,1)}, bf16[4096,384]{1,0:T(8,128)(2,1)}, bf16[384,4096]{1,0:T(8,128)(2,1)}) custom-call(bf16[3072,2048]{1,0:T(8,128)(2,1)} %bitcast.25, bf16[3072,2048]{1,0:T(8,128)(2,1)} %bitcast.26, bf16[768,384]{1,0:T(8,128)(2,1)} %get-tuple-element.57.h_ref, bf16[768,768]{1,0:T(8,128)(2,1)} %get-tuple-element.52.a_ref), custom_call_target="tpu_custom_call" | custom-call | flops 7247757312 | bytes 22020096 | tf_op jit(solution)/shard_map/pallas_call | solution.py:407
  250.0 58.0 %all-to-all-done.3 = bf16[128,24,1024]{2,1,0:T(8,128)(2,1)} async-done(((bf16[128,24,1024]{2,1,0:T(8,128)(2,1)}), bf16[128,24,1024]{2,1,0:T(8,128)(2,1)}, u32[]{:S(2)}, u32[]{:S(2)}) %all-to-all-start.3) | async-done | bytes 6291488 | tf_op jit(solution)/shard_map/all_to_all | solution.py:404
  308.0 6.1 %shard_map.153 = (bf16[512,1024]{1,0:T(8,128)(2,1)}, bf16[1024,128]{1,0:T(8,128)(2,1)}) custom-call(bf16[512,1536]{1,0:T(8,128)(2,1)} %shard_map.151.mt_ref, bf16[4,768,1024]{2,1,0:T(8,128)(2,1)} %bitcast.12.ret_ref, bf16[512,1024]{1,0:T(8,128)(2,1)} %get-tuple-element.63.og_ref, bf16[512,1024]{1,0:T(8,128)(2,1)} %q_ref.5), custom_call_target="tpu_custom_call" | custom-call | flops 1610612736 | bytes 11010048 | tf_op jit(solution)/shard_map/pallas_call | solution.py:433
  314.1 7.5 %all-to-all-start.4 = ((bf16[32,32,128]{2,1,0:T(8,128)(2,1)}), bf16[32,32,128]{2,1,0:T(8,128)(2,1)S(1)}, u32[]{:S(2)}, u32[]{:S(2)}) async-start(bf16[32,32,128]{2,1,0:T(8,128)(2,1)} %bitcast.30), calls=%async_computation.4 | async-start | bytes 524288 | tf_op jit(solution)/shard_map/all_to_all | solution.py:328
  321.6 7.6 %shard_map.155 = (f32[512,1024]{1,0:T(8,128)}, f32[512,1024]{1,0:T(8,128)}) custom-call(bf16[512,1024]{1,0:T(8,128)(2,1)} %q_ref.5, bf16[512,1024]{1,0:T(8,128)(2,1)} %get-tuple-element.41.mk_ref, bf16[512,1024]{1,0:T(8,128)(2,1)} %v_ref.9, bf16[512,1024]{1,0:T(8,128)(2,1)} %get-tuple-element.64.ag_ref), custom_call_target="tpu_custom_call" | custom-call | flops 2147483648 | bytes 8388608 | tf_op jit(solution)/shard_map/pallas_call | solution.py:439
  329.2 0.0 copy-start
  329.2 0.0 copy-start.3
  329.2 1.4 all-to-all-done.4.x_ref
  330.6 0.9 shard_map.156
  331.4 6.0 %all-to-all-start.5 = ((bf16[32,32,128]{2,1,0:T(8,128)(2,1)}), bf16[32,32,128]{2,1,0:T(8,128)(2,1)S(1)}, u32[]{:S(2)}, u32[]{:S(2)}) async-start(bf16[32,32,128]{2,1,0:T(8,128)(2,1)} %shard_map.156), calls=%async_computation.5 | async-start | bytes 524288 | tf_op jit(solution)/shard_map/all_to_all | solution.py:334
  337.4 5.0 %shard_map.154 = bf16[512,1024]{1,0:T(8,128)(2,1)} custom-call(bf16[512,1024]{1,0:T(8,128)(2,1)} %get-tuple-element.41.mk_ref, bf16[512,1024]{1,0:T(8,128)(2,1)} %v_ref.9, bf16[512,1024]{1,0:T(8,128)(2,1)} %get-tuple-element.64.ag_ref, bf16[1024,128]{1,0:T(8,128)(2,1)} %bitcast.19), custom_call_target="tpu_custom_call" | custom-call | flops 1073741824 | bytes 4194304 | tf_op jit(solution)/shard_map/pallas_call | solution.py:444
  342.5 4.0 %all-to-all-done.5 = bf16[32,32,128]{2,1,0:T(8,128)(2,1)S(1)} async-done(((bf16[32,32,128]{2,1,0:T(8,128)(2,1)}), bf16[32,32,128]{2,1,0:T(8,128)(2,1)S(1)}, u32[]{:S(2)}, u32[]{:S(2)}) %all-to-all-start.5) | async-done | bytes 262176 | tf_op jit(solution)/shard_map/all_to_all | solution.py:334
  346.4 0.0 copy-done
  346.4 0.0 copy-done.3
  346.4 4.2 %shard_map.157 = (bf16[512,1024]{1,0:T(8,128)(2,1)}, bf16[512,1024]{1,0:T(8,128)(2,1)}) custom-call(bf16[512,1024]{1,0:T(8,128)(2,1)S(1)} %copy-done, bf16[512,1024]{1,0:T(8,128)(2,1)} %v_ref.9, s32[8,512]{1,0:T(8,128)S(1)} %bitcast.22, bf16[1024,128]{1,0:T(8,128)(2,1)S(1)} %bitcast.20, f32[512,1024]{1,0:T(8,128)} %get-tuple-element.69.gki_ref, ...), custom_call_target="tpu_custom_call" | custom-call | flops 268435456 | bytes 8388608 | tf_op jit(solution)/shard_map/pallas_call | solution.py:448
Async XLA Ops:
  3.8 18.6 %all-to-all-start = ((bf16[32,32,128]{2,1,0:T(8,128)(2,1)}), bf16[32,32,128]{2,1,0:T(8,128)(2,1)S(1)}, u32[]{:S(2)}, u32[]{:S(2)}) async-start(bf16[32,32,128]{2,1,0:T(8,128)(2,1)} %bitcast.29), calls=%async_computation | async-start | bytes 524288 | tf_op jit(solution)/shard_map/all_to_all | solution.py:328
  15.8 14.1 %collective-permute-start = (bf16[144,1024]{1,0:T(8,128)(2,1)}, bf16[144,1024]{1,0:T(8,128)(2,1)S(1)}, u32[]{:S(2)}, u32[]{:S(2)}) collective-permute-start(bf16[144,1024]{1,0:T(8,128)(2,1)} %get-tuple-element.45), channel_id=1, source_target_pairs={{0,1},{1,2},{2,3},{3,0},{4,5},{5,6},{6,7},{7,4},{8,9},{9,10},{10,1... | collective-permute-start | bytes 884744 | tf_op jit(solution)/shard_map/ppermute | solution.py:352
  17.0 15.9 %collective-permute-start.1 = (bf16[144,1024]{1,0:T(8,128)(2,1)}, bf16[144,1024]{1,0:T(8,128)(2,1)S(1)}, u32[]{:S(2)}, u32[]{:S(2)}) collective-permute-start(bf16[144,1024]{1,0:T(8,128)(2,1)} %get-tuple-element.46), channel_id=1, source_target_pairs={{0,2},{1,3},{2,0},{3,1},{4,6},{5,7},{6,4},{7,5},{8,10},{9,11},{10,... | collective-permute-start | bytes 884744 | tf_op jit(solution)/shard_map/ppermute | solution.py:352
  19.5 13.4 %collective-permute-start.2 = (bf16[144,1024]{1,0:T(8,128)(2,1)}, bf16[144,1024]{1,0:T(8,128)(2,1)S(1)}, u32[]{:S(2)}, u32[]{:S(2)}) collective-permute-start(bf16[144,1024]{1,0:T(8,128)(2,1)} %get-tuple-element.47), channel_id=1, source_target_pairs={{0,3},{1,0},{2,1},{3,2},{4,7},{5,4},{6,5},{7,6},{8,11},{9,8},{10,9... | collective-permute-start | bytes 884744 | tf_op jit(solution)/shard_map/ppermute | solution.py:352
  23.3 17.1 %copy-start.1 = (bf16[512,1024]{1,0:T(8,128)(2,1)S(1)}, bf16[512,1024]{1,0:T(8,128)(2,1)}, u32[]{:S(2)}) copy-start(bf16[512,1024]{1,0:T(8,128)(2,1)} %q_ref.5) | copy-start | bytes 3145732
  23.3 17.1 %all-to-all-start.1 = ((bf16[32,32,128]{2,1,0:T(8,128)(2,1)}), bf16[32,32,128]{2,1,0:T(8,128)(2,1)S(1)}, u32[]{:S(2)}, u32[]{:S(2)}) async-start(bf16[32,32,128]{2,1,0:T(8,128)(2,1)} %shard_map.148), calls=%async_computation.1 | async-start | bytes 524288 | tf_op jit(solution)/shard_map/all_to_all | solution.py:334
  29.9 3.0 copy-start.4
  32.9 0.7 copy-start.5
  32.9 0.8 copy-start.6
  40.4 8.2 %copy-start.2 = (bf16[32,32,128]{2,1,0:T(8,128)(2,1)}, bf16[32,32,128]{2,1,0:T(8,128)(2,1)S(1)}, u32[]{:S(2)}) copy-start(bf16[32,32,128]{2,1,0:T(8,128)(2,1)S(1)} %all-to-all-done.1) | copy-start | bytes 786436
  224.7 83.3 %all-to-all-start.3 = ((bf16[128,24,1024]{2,1,0:T(8,128)(2,1)}), bf16[128,24,1024]{2,1,0:T(8,128)(2,1)}, u32[]{:S(2)}, u32[]{:S(2)}) async-start(bf16[128,24,1024]{2,1,0:T(8,128)(2,1)} %bitcast.28), calls=%async_computation.3 | async-start | bytes 12582912 | tf_op jit(solution)/shard_map/all_to_all | solution.py:404
  314.1 16.5 %all-to-all-start.4 = ((bf16[32,32,128]{2,1,0:T(8,128)(2,1)}), bf16[32,32,128]{2,1,0:T(8,128)(2,1)S(1)}, u32[]{:S(2)}, u32[]{:S(2)}) async-start(bf16[32,32,128]{2,1,0:T(8,128)(2,1)} %bitcast.30), calls=%async_computation.4 | async-start | bytes 524288 | tf_op jit(solution)/shard_map/all_to_all | solution.py:328
  329.2 17.3 %copy-start = (bf16[512,1024]{1,0:T(8,128)(2,1)S(1)}, bf16[512,1024]{1,0:T(8,128)(2,1)}, u32[]{:S(2)}) copy-start(bf16[512,1024]{1,0:T(8,128)(2,1)} %get-tuple-element.41.mk_ref) | copy-start | bytes 3145732
  329.2 17.3 %copy-start.3 = (s32[512,8]{0,1:T(8,128)S(1)}, s32[512,8]{0,1:T(8,128)}, u32[]{:S(2)}) copy-start(s32[512,8]{0,1:T(8,128)} %param.13) | copy-start | bytes 49156
  331.4 15.0 %all-to-all-start.5 = ((bf16[32,32,128]{2,1,0:T(8,128)(2,1)}), bf16[32,32,128]{2,1,0:T(8,128)(2,1)S(1)}, u32[]{:S(2)}, u32[]{:S(2)}) async-start(bf16[32,32,128]{2,1,0:T(8,128)(2,1)} %shard_map.156), calls=%async_computation.5 | async-start | bytes 524288 | tf_op jit(solution)/shard_map/all_to_all | solution.py:334

commit v4 on v3

--- a/solution.py
+++ b/solution.py
@@ -100,10 +100,8 @@
                 hit0, pack[2:3], jnp.where(hit1, pack[5:6], 0.0)
             ).astype(BF16)
 
-    @pl.when(step > 0)
-    def _():
-        cols = pl.ds(pl.multiple_of((step - 1) * pair, pair), pair)
-        put_rows(w_ref, g_ref[:, cols], o_ref)
+    cols = pl.ds(pl.multiple_of(step * pair, pair), pair)
+    put_rows(w_ref, g_ref[:, cols], o_ref)
 
 
 def state_body(head, k_ref, v_ref, s_ref, bs_ref, mk_ref):
@@ -117,6 +115,17 @@
         bs_ref[cols, :] = mm(masked[:, cols], value[:, cols], TN).astype(BF16)
 
 
+def intra_body(head, q_ref, mk_ref, v_ref, o_ref):
+    length, width = q_ref.shape
+    t = lax.broadcasted_iota(jnp.int32, (length, length), 0)
+    s = lax.broadcasted_iota(jnp.int32, (length, length), 1)
+    for h in range(width // head):
+        cols = slice(h * head, (h + 1) * head)
+        scores = mm(q_ref[:, cols], mk_ref[:, cols], NT)
+        scores = jnp.where(t >= s, scores, 0.0).astype(BF16)
+        o_ref[:, cols] = mm(scores, v_ref[:, cols])
+
+
 def sum_body(reverse, x_ref, o_ref):
     count = x_ref.shape[0]
 
@@ -125,7 +134,7 @@
         o_ref[at] = total.astype(BF16)
         return total + x_ref[at].astype(F32)
 
-    lax.fori_loop(0, count, step, jnp.zeros(x_ref.shape[1:], F32))
+    lax.fori_loop(0, count, step, jnp.zeros(x_ref.shape[1:], F32), unroll=True)
 
 
 def select_t_body(count, mine_ref, *refs):
@@ -155,17 +164,13 @@
         o_ref[p, 1] = picked
 
 
-def rows_body(head, scaling, m_ref, q_ref, mk_ref, v_ref, s_ref, buf_ref, o_ref):
+def rows_body(head, scaling, m_ref, q_ref, intra_ref, s_ref, buf_ref, o_ref):
     del buf_ref
-    length, width = q_ref.shape
-    t = lax.broadcasted_iota(jnp.int32, (length, length), 0)
-    s = lax.broadcasted_iota(jnp.int32, (length, length), 1)
+    width = q_ref.shape[1]
     parts = []
     for h in range(width // head):
         cols = slice(h * head, (h + 1) * head)
-        scores = mm(q_ref[:, cols], mk_ref[:, cols], NT)
-        scores = jnp.where(t >= s, scores, 0.0).astype(BF16)
-        total = mm(scores, v_ref[:, cols]) + mm(q_ref[:, cols], s_ref[cols, :])
+        total = intra_ref[:, cols] + mm(q_ref[:, cols], s_ref[cols, :])
         parts.append((scaling * total).astype(BF16))
     put_rows(m_ref, jnp.concatenate(parts, axis=1), o_ref)
 
@@ -176,7 +181,7 @@
     i = pl.program_id(0)
     rows, hidden = hid.shape
     width = r_ref.shape[1]
-    chunk = rows // 6
+    chunk = rows // 3
     part = pl.ds(pl.multiple_of(lax.rem(i, steps) * width, width), width)
 
     @pl.when(i < steps)
@@ -189,17 +194,18 @@
         both[...] = mm(r_ref[...], cat[part, :])
         hid[...] = mm(g_ref[...], wd_ref[...], NT)
 
-    @pl.when((i > 0) & (i < steps))
+    @pl.when((i > 0) & (i < steps - 1))
     def _():
         both[...] += mm(r_ref[...], cat[part, :])
         hid[...] += mm(g_ref[...], wd_ref[...], NT)
 
     @pl.when(i == steps - 1)
     def _():
-        @pl.loop(0, rows // chunk)
-        def _(c):
-            at = pl.ds(pl.multiple_of(c * chunk, chunk), chunk)
-            g, u, d = both[at, :hidden], both[at, hidden:], hid[at, :]
+        for c in range(rows // chunk):
+            at = slice(c * chunk, (c + 1) * chunk)
+            total = both[at, :] + mm(r_ref[at, :], cat[part, :])
+            d = hid[at, :] + mm(g_ref[at, :], wd_ref[...], NT)
+            g, u = total[:, :hidden], total[:, hidden:]
             sig = jax.nn.sigmoid(g)
             silu = g * sig
             h_ref[at, :] = (silu * u).astype(BF16)
@@ -348,31 +354,33 @@
         [smem, whole(tokens, model), whole(top, tokens), whole(top, tokens)],
         [whole(*piece)] * exp, [shape(*piece)] * exp, 1e6, 2 * unit,
     )(mine, own_grad, routes.T, route_probs.T)
-    pieces = [pieces[0]] + [
-        lax.ppermute(pieces[i], "exp", [(j, (j + i) % exp) for j in range(exp)])
-        for i in range(1, exp)
-    ]
+    pieces = list(pieces)
+    for i in sorted(range(1, exp), key=lambda i: -min(i, exp - i)):
+        pieces[i] = lax.ppermute(pieces[i], "exp", [(j, (j + i) % exp) for j in range(exp)])
     states_in, _ = exchange(block_state, False, ())
+    intra = call(
+        functools.partial(intra_body, head), (pairs,), [wide] * 3, wide, seq32,
+        4 * length * length * width, 5 * unit,
+    )(queries, masked, value_vectors)
+
     send_shape = shape(2, 2, half_rows, 2 * width)
     send_flops = 2 * rows * length * width
     send_bytes = 4 * rows * width + 2 * rows * length + 2 * unit
     grad_cols, select, buffer = call(
-        functools.partial(prepare_body, exp), (1 + pairs,), [smem] + [whole(*piece)] * exp,
+        functools.partial(prepare_body, exp), (pairs,), [smem] + [whole(*piece)] * exp,
         [
             whole(length, width), whole(rows, length),
-            pl.BlockSpec(
-                (2, 2, half_rows, pair), lambda i: (0, 0, 0, jnp.maximum(i - 1, 0) + pairs)
-            ),
+            pl.BlockSpec((2, 2, half_rows, pair), lambda i: (0, 0, 0, i + pairs)),
         ],
         [seq, shape(rows, length), send_shape], send_flops, send_bytes,
         scratch_shapes=[pltpu.VMEM((rows, length), BF16)],
     )(mine, *pieces)
     buffer = call(
         functools.partial(rows_body, head, scaling), (pairs,),
-        [whole(rows, length), wide, wide, wide, tall, pl.BlockSpec(memory_space=pl.ANY)],
+        [whole(rows, length), wide, wide, tall, pl.BlockSpec(memory_space=pl.ANY)],
         pl.BlockSpec((2, 2, half_rows, pair), lambda i: (0, 0, 0, i)),
-        send_shape, send_flops, send_bytes, 52, input_output_aliases={5: 0},
-    )(select, queries, masked, value_vectors, states_in, buffer)
+        send_shape, send_flops, send_bytes, 52, input_output_aliases={4: 0},
+    )(select, queries, intra, states_in, buffer)
     got = lax.all_to_all(
         buffer.reshape(devices, slots, 2 * width), everywhere, 0, 0, tiled=True
     ).reshape(exp * half_rows, 2 * width)

time: 351 us -> 349 us (level)
    pallas_call x1 -> x2, Pallas kernels: 6.69 us -> 11.7 us  [the longest x1 6.65 us: on_device(): call(functools.partial(prepare_body, exp), (pairs,), [smem] + [whole(*pie...]
  transfers between devices with their start and end apart: 8 -> 8, of which waited for: 5 -> 4; matrix products, arithmetic and copies ran while one was open for 0% -> 0% of each run, Pallas kernels for 11% -> 13%
where the time goes in v4:
time: 349 us; the launch traced here: 348 us
  blocking collectives  153 us (44%)
  Pallas kernels  85.5 us (24%)
  waiting for transfers between devices  65.1 us (19%)
  starting transfers between devices  42.7 us (12%)
    all_to_all x1, blocking collectives, on_device(): lax.all_to_all(buffer.reshape(devices, slots, 2 * width), everywhere, 0,...  153 us
    all_to_all x1, waiting for transfers between devices, on_device(): lax.all_to_all(back_rows.reshape(devices, slots, width), everywhere, 0, 0...  58 us
    all_to_all x4, starting transfers between devices, exchange(): pieces = lax.all_to_all(pieces, 'ctx', 0, 0, tiled=True)  29.5 us
    pallas_call x1, Pallas kernels, on_device(): call(functools.partial(expert_body, exp), (2 * exp,), [pl.BlockSpec((half...  20.3 us
    pallas_call x1, Pallas kernels, on_device(): call(weights_body, (exp,), [pl.BlockSpec((half_rows, width), lambda i: (i...  14.7 us
    all_to_all x1, starting transfers between devices, on_device(): lax.all_to_all(back_rows.reshape(devices, slots, width), everywhere, 0, 0...  8.37 us
    pallas_call x1, Pallas kernels, on_device(): call(functools.partial(back_body, head, scaling), (pairs,), [wide] * 4, [...  7.59 us
    all_to_all x4, waiting for transfers between devices, exchange(): pieces = lax.all_to_all(pieces, 'ctx', 0, 0, tiled=True)  7.14 us
  transfers between devices with their start and end apart: 8, of which 4 were waited for; matrix products, arithmetic and copies ran while one was open for 0% of the time, Pallas kernels for 13%

profile of v4, /device:TPU:1, one launch (start us, length us, event | category | flops | bytes accessed | tf_op | source)
XLA Modules:
  0.0 348.5 jit_solution(2869438668192181220)
XLA Ops:
  0.6 3.2 shard_map.145
  3.8 9.6 %all-to-all-start = ((bf16[32,32,128]{2,1,0:T(8,128)(2,1)}), bf16[32,32,128]{2,1,0:T(8,128)(2,1)S(1)}, u32[]{:S(2)}, u32[]{:S(2)}) async-start(bf16[32,32,128]{2,1,0:T(8,128)(2,1)} %bitcast.29), calls=%async_computation | async-start | bytes 524288 | tf_op jit(solution)/shard_map/all_to_all | solution.py:334
  13.4 2.4 shard_map.146
  15.8 1.2 collective-permute-start
  17.0 2.5 collective-permute-start.1
  19.5 1.2 collective-permute-start.2
  20.6 1.8 all-to-all-done.x_ref
  22.4 0.8 shard_map.149
  23.2 6.4 %all-to-all-start.1 = ((bf16[32,32,128]{2,1,0:T(8,128)(2,1)}), bf16[32,32,128]{2,1,0:T(8,128)(2,1)S(1)}, u32[]{:S(2)}, u32[]{:S(2)}) async-start(bf16[32,32,128]{2,1,0:T(8,128)(2,1)} %shard_map.149), calls=%async_computation.1 | async-start | bytes 524288 | tf_op jit(solution)/shard_map/all_to_all | solution.py:340
  29.6 5.1 %shard_map.148.intra_ref = f32[512,1024]{1,0:T(8,128)} custom-call(bf16[512,1024]{1,0:T(8,128)(2,1)} %q_ref.7, bf16[512,1024]{1,0:T(8,128)(2,1)} %get-tuple-element.41.mk_ref, bf16[512,1024]{1,0:T(8,128)(2,1)} %v_ref.9), custom_call_target="tpu_custom_call" | custom-call | flops 1073741824 | bytes 5242880 | tf_op jit(solution)/shard_map/pallas_call | solution.py:361
  34.7 0.0 copy-start
  34.7 0.0 collective-permute-done.refs_1_
  34.7 0.0 copy-start.4
  34.7 0.0 collective-permute-done.1.refs_2_
  34.7 0.0 copy-start.5
  34.7 0.0 collective-permute-done.2.refs_3_
  34.7 0.0 copy-start.6
  34.7 0.7 copy-done.4
  35.4 0.1 copy-done.5
  35.5 0.1 copy-done.6
  35.6 6.7 %shard_map.147 = (bf16[512,1024]{1,0:T(8,128)(2,1)}, bf16[1536,512]{1,0:T(8,128)(2,1)}, bf16[2,2,768,2048]{3,2,1,0:T(8,128)(2,1)}) custom-call(s32[1]{0:T(128)} %bitcast.1.mine_ref, bf16[144,1024]{1,0:T(8,128)(2,1)} %get-tuple-element.53.refs_0_, bf16[144,1024]{1,0:T(8,128)(2,1)} %copy-done.4, bf16[144,1024]{1,0:T(8,128)(2,1)} %copy-done.5, ...), custom_call_target="tpu_custom_call" | custom-call | flops 1610612736 | bytes 9961472 | tf_op jit(solution)/shard_map/pallas_call | solution.py:369
  42.3 0.0 all-to-all-done.1
  42.3 0.0 copy-start.2
  42.3 0.0 copy-done
  42.3 6.0 %shard_map.150 = bf16[2,2,768,2048]{3,2,1,0:T(8,128)(2,1)} custom-call(bf16[1536,512]{1,0:T(8,128)(2,1)} %get-tuple-element.48.m_ref, bf16[512,1024]{1,0:T(8,128)(2,1)S(1)} %copy-done, f32[512,1024]{1,0:T(8,128)} %shard_map.148.intra_ref, bf16[1024,128]{1,0:T(8,128)(2,1)S(1)} %bitcast.18, ...), custom_call_target="tpu_custom_call", output_to_operand_aliasing={{}: (4, {})} | custom-call | flops 1610612736 | bytes 9961472 | tf_op jit(solution)/shard_map/pallas_call | solution.py:378
  48.3 0.0 copy-done.2
  48.3 153.5 %all_to_all.30 = bf16[128,24,2048]{2,1,0:T(8,128)(2,1)} all-to-all(bf16[128,24,2048]{2,1,0:T(8,128)(2,1)} %bitcast.27), channel_id=1, replica_groups=mesh['ctx'=32,'exp'=4] {'exp','ctx'}, dimensions={0} | all-to-all | bytes 25165824 | tf_op jit(solution)/shard_map/all_to_all | solution.py:384
  201.8 20.3 %shard_map.151 = (bf16[3072,1024]{1,0:T(8,128)(2,1)}, bf16[768,384]{1,0:T(8,128)(2,1)}, bf16[768,768]{1,0:T(8,128)(2,1)}) custom-call(bf16[3072,2048]{1,0:T(8,128)(2,1)} %bitcast.23, bf16[3072,2048]{1,0:T(8,128)(2,1)} %bitcast.24, bf16[4096,384]{1,0:T(8,128)(2,1)} %bitcast.33, bf16[4096,384]{1,0:T(8,128)(2,1)} %bitcast.34, bf16[384,4096]{1,0:T(8,128)(2,1)} %bitcast.35), custom_call_target="tpu_custom_call" | custom-call | flops 12079595520 | bytes 34603008 | tf_op jit(solution)/shard_map/pallas_call | solution.py:391
  222.1 8.4 %all-to-all-start.3 = ((bf16[128,24,1024]{2,1,0:T(8,128)(2,1)}), bf16[128,24,1024]{2,1,0:T(8,128)(2,1)}, u32[]{:S(2)}, u32[]{:S(2)}) async-start(bf16[128,24,1024]{2,1,0:T(8,128)(2,1)} %bitcast.28), calls=%async_computation.3 | async-start | bytes 12582912 | tf_op jit(solution)/shard_map/all_to_all | solution.py:412
  230.4 2.9 shard_map.152.mt_ref
  233.4 14.7 %shard_map.153 = (bf16[4096,384]{1,0:T(8,128)(2,1)}, bf16[4096,384]{1,0:T(8,128)(2,1)}, bf16[384,4096]{1,0:T(8,128)(2,1)}) custom-call(bf16[3072,2048]{1,0:T(8,128)(2,1)} %bitcast.25, bf16[3072,2048]{1,0:T(8,128)(2,1)} %bitcast.26, bf16[768,384]{1,0:T(8,128)(2,1)} %get-tuple-element.57.h_ref, bf16[768,768]{1,0:T(8,128)(2,1)} %get-tuple-element.52.a_ref), custom_call_target="tpu_custom_call" | custom-call | flops 7247757312 | bytes 22020096 | tf_op jit(solution)/shard_map/pallas_call | solution.py:415
  248.0 58.0 %all-to-all-done.3 = bf16[128,24,1024]{2,1,0:T(8,128)(2,1)} async-done(((bf16[128,24,1024]{2,1,0:T(8,128)(2,1)}), bf16[128,24,1024]{2,1,0:T(8,128)(2,1)}, u32[]{:S(2)}, u32[]{:S(2)}) %all-to-all-start.3) | async-done | bytes 6291488 | tf_op jit(solution)/shard_map/all_to_all | solution.py:412
  306.0 6.1 %shard_map.154 = (bf16[512,1024]{1,0:T(8,128)(2,1)}, bf16[1024,128]{1,0:T(8,128)(2,1)}) custom-call(bf16[512,1536]{1,0:T(8,128)(2,1)} %shard_map.152.mt_ref, bf16[4,768,1024]{2,1,0:T(8,128)(2,1)} %bitcast.12.ret_ref, bf16[512,1024]{1,0:T(8,128)(2,1)} %get-tuple-element.63.og_ref, bf16[512,1024]{1,0:T(8,128)(2,1)} %q_ref.7), custom_call_target="tpu_custom_call" | custom-call | flops 1610612736 | bytes 11010048 | tf_op jit(solution)/shard_map/pallas_call | solution.py:441
  312.1 7.5 %all-to-all-start.4 = ((bf16[32,32,128]{2,1,0:T(8,128)(2,1)}), bf16[32,32,128]{2,1,0:T(8,128)(2,1)S(1)}, u32[]{:S(2)}, u32[]{:S(2)}) async-start(bf16[32,32,128]{2,1,0:T(8,128)(2,1)} %bitcast.30), calls=%async_computation.4 | async-start | bytes 524288 | tf_op jit(solution)/shard_map/all_to_all | solution.py:334
  319.5 7.6 %shard_map.156 = (f32[512,1024]{1,0:T(8,128)}, f32[512,1024]{1,0:T(8,128)}) custom-call(bf16[512,1024]{1,0:T(8,128)(2,1)} %q_ref.7, bf16[512,1024]{1,0:T(8,128)(2,1)} %get-tuple-element.41.mk_ref, bf16[512,1024]{1,0:T(8,128)(2,1)} %v_ref.9, bf16[512,1024]{1,0:T(8,128)(2,1)} %get-tuple-element.64.ag_ref), custom_call_target="tpu_custom_call" | custom-call | flops 2147483648 | bytes 8388608 | tf_op jit(solution)/shard_map/pallas_call | solution.py:447
  327.1 0.0 copy-start.1
  327.1 0.0 copy-start.3
  327.1 1.4 all-to-all-done.4.x_ref
  328.5 0.7 shard_map.157
  329.3 6.0 %all-to-all-start.5 = ((bf16[32,32,128]{2,1,0:T(8,128)(2,1)}), bf16[32,32,128]{2,1,0:T(8,128)(2,1)S(1)}, u32[]{:S(2)}, u32[]{:S(2)}) async-start(bf16[32,32,128]{2,1,0:T(8,128)(2,1)} %shard_map.157), calls=%async_computation.5 | async-start | bytes 524288 | tf_op jit(solution)/shard_map/all_to_all | solution.py:340
  335.3 5.0 %shard_map.155 = bf16[512,1024]{1,0:T(8,128)(2,1)} custom-call(bf16[512,1024]{1,0:T(8,128)(2,1)} %get-tuple-element.41.mk_ref, bf16[512,1024]{1,0:T(8,128)(2,1)} %v_ref.9, bf16[512,1024]{1,0:T(8,128)(2,1)} %get-tuple-element.64.ag_ref, bf16[1024,128]{1,0:T(8,128)(2,1)} %bitcast.19), custom_call_target="tpu_custom_call" | custom-call | flops 1073741824 | bytes 4194304 | tf_op jit(solution)/shard_map/pallas_call | solution.py:452
  340.3 4.0 %all-to-all-done.5 = bf16[32,32,128]{2,1,0:T(8,128)(2,1)S(1)} async-done(((bf16[32,32,128]{2,1,0:T(8,128)(2,1)}), bf16[32,32,128]{2,1,0:T(8,128)(2,1)S(1)}, u32[]{:S(2)}, u32[]{:S(2)}) %all-to-all-start.5) | async-done | bytes 262176 | tf_op jit(solution)/shard_map/all_to_all | solution.py:340
  344.3 0.0 copy-done.1
  344.3 0.0 copy-done.3
  344.3 4.2 %shard_map.158 = (bf16[512,1024]{1,0:T(8,128)(2,1)}, bf16[512,1024]{1,0:T(8,128)(2,1)}) custom-call(bf16[512,1024]{1,0:T(8,128)(2,1)S(1)} %copy-done.1, bf16[512,1024]{1,0:T(8,128)(2,1)} %v_ref.9, s32[8,512]{1,0:T(8,128)S(1)} %bitcast.22, bf16[1024,128]{1,0:T(8,128)(2,1)S(1)} %bitcast.20, f32[512,1024]{1,0:T(8,128)} %get-tuple-element.69.gki_ref, ...), custom_call_target="tpu_custom_call" | custom-call | flops 268435456 | bytes 8388608 | tf_op jit(solution)/shard_map/pallas_call | solution.py:456
Async XLA Ops:
  3.8 18.6 %all-to-all-start = ((bf16[32,32,128]{2,1,0:T(8,128)(2,1)}), bf16[32,32,128]{2,1,0:T(8,128)(2,1)S(1)}, u32[]{:S(2)}, u32[]{:S(2)}) async-start(bf16[32,32,128]{2,1,0:T(8,128)(2,1)} %bitcast.29), calls=%async_computation | async-start | bytes 524288 | tf_op jit(solution)/shard_map/all_to_all | solution.py:334
  15.8 18.9 %collective-permute-start = (bf16[144,1024]{1,0:T(8,128)(2,1)}, bf16[144,1024]{1,0:T(8,128)(2,1)S(1)}, u32[]{:S(2)}, u32[]{:S(2)}) collective-permute-start(bf16[144,1024]{1,0:T(8,128)(2,1)} %get-tuple-element.45), channel_id=1, source_target_pairs={{0,1},{1,2},{2,3},{3,0},{4,5},{5,6},{6,7},{7,4},{8,9},{9,10},{10,1... | collective-permute-start | bytes 884744 | tf_op jit(solution)/shard_map/ppermute | solution.py:359
  17.0 17.7 %collective-permute-start.1 = (bf16[144,1024]{1,0:T(8,128)(2,1)}, bf16[144,1024]{1,0:T(8,128)(2,1)S(1)}, u32[]{:S(2)}, u32[]{:S(2)}) collective-permute-start(bf16[144,1024]{1,0:T(8,128)(2,1)} %get-tuple-element.46), channel_id=1, source_target_pairs={{0,2},{1,3},{2,0},{3,1},{4,6},{5,7},{6,4},{7,5},{8,10},{9,11},{10,... | collective-permute-start | bytes 884744 | tf_op jit(solution)/shard_map/ppermute | solution.py:359
  19.5 15.3 %collective-permute-start.2 = (bf16[144,1024]{1,0:T(8,128)(2,1)}, bf16[144,1024]{1,0:T(8,128)(2,1)S(1)}, u32[]{:S(2)}, u32[]{:S(2)}) collective-permute-start(bf16[144,1024]{1,0:T(8,128)(2,1)} %get-tuple-element.47), channel_id=1, source_target_pairs={{0,3},{1,0},{2,1},{3,2},{4,7},{5,4},{6,5},{7,6},{8,11},{9,8},{10,9... | collective-permute-start | bytes 884744 | tf_op jit(solution)/shard_map/ppermute | solution.py:359
  23.2 19.1 %all-to-all-start.1 = ((bf16[32,32,128]{2,1,0:T(8,128)(2,1)}), bf16[32,32,128]{2,1,0:T(8,128)(2,1)S(1)}, u32[]{:S(2)}, u32[]{:S(2)}) async-start(bf16[32,32,128]{2,1,0:T(8,128)(2,1)} %shard_map.149), calls=%async_computation.1 | async-start | bytes 524288 | tf_op jit(solution)/shard_map/all_to_all | solution.py:340
  34.7 7.6 %copy-start = (bf16[512,1024]{1,0:T(8,128)(2,1)S(1)}, bf16[512,1024]{1,0:T(8,128)(2,1)}, u32[]{:S(2)}) copy-start(bf16[512,1024]{1,0:T(8,128)(2,1)} %q_ref.7) | copy-start | bytes 3145732
  34.7 0.7 copy-start.4
  34.7 0.8 copy-start.5
  34.7 0.9 copy-start.6
  42.3 6.0 %copy-start.2 = (bf16[32,32,128]{2,1,0:T(8,128)(2,1)}, bf16[32,32,128]{2,1,0:T(8,128)(2,1)S(1)}, u32[]{:S(2)}) copy-start(bf16[32,32,128]{2,1,0:T(8,128)(2,1)S(1)} %all-to-all-done.1) | copy-start | bytes 786436
  222.1 83.9 %all-to-all-start.3 = ((bf16[128,24,1024]{2,1,0:T(8,128)(2,1)}), bf16[128,24,1024]{2,1,0:T(8,128)(2,1)}, u32[]{:S(2)}, u32[]{:S(2)}) async-start(bf16[128,24,1024]{2,1,0:T(8,128)(2,1)} %bitcast.28), calls=%async_computation.3 | async-start | bytes 12582912 | tf_op jit(solution)/shard_map/all_to_all | solution.py:412
  312.1 16.5 %all-to-all-start.4 = ((bf16[32,32,128]{2,1,0:T(8,128)(2,1)}), bf16[32,32,128]{2,1,0:T(8,128)(2,1)S(1)}, u32[]{:S(2)}, u32[]{:S(2)}) async-start(bf16[32,32,128]{2,1,0:T(8,128)(2,1)} %bitcast.30), calls=%async_computation.4 | async-start | bytes 524288 | tf_op jit(solution)/shard_map/all_to_all | solution.py:334
  327.1 17.1 %copy-start.1 = (bf16[512,1024]{1,0:T(8,128)(2,1)S(1)}, bf16[512,1024]{1,0:T(8,128)(2,1)}, u32[]{:S(2)}) copy-start(bf16[512,1024]{1,0:T(8,128)(2,1)} %get-tuple-element.41.mk_ref) | copy-start | bytes 3145732
  327.1 17.1 %copy-start.3 = (s32[512,8]{0,1:T(8,128)S(1)}, s32[512,8]{0,1:T(8,128)}, u32[]{:S(2)}) copy-start(s32[512,8]{0,1:T(8,128)} %param.13) | copy-start | bytes 49156
  329.3 15.0 %all-to-all-start.5 = ((bf16[32,32,128]{2,1,0:T(8,128)(2,1)}), bf16[32,32,128]{2,1,0:T(8,128)(2,1)S(1)}, u32[]{:S(2)}, u32[]{:S(2)}) async-start(bf16[32,32,128]{2,1,0:T(8,128)(2,1)} %shard_map.157), calls=%async_computation.5 | async-start | bytes 524288 | tf_op jit(solution)/shard_map/all_to_all | solution.py:340

commit v5 on v4

--- a/solution.py
+++ b/solution.py
@@ -123,7 +123,7 @@
         cols = slice(h * head, (h + 1) * head)
         scores = mm(q_ref[:, cols], mk_ref[:, cols], NT)
         scores = jnp.where(t >= s, scores, 0.0).astype(BF16)
-        o_ref[:, cols] = mm(scores, v_ref[:, cols])
+        o_ref[:, cols] = mm(scores, v_ref[:, cols]).astype(BF16)
 
 
 def sum_body(reverse, x_ref, o_ref):
@@ -170,7 +170,7 @@
     parts = []
     for h in range(width // head):
         cols = slice(h * head, (h + 1) * head)
-        total = intra_ref[:, cols] + mm(q_ref[:, cols], s_ref[cols, :])
+        total = intra_ref[:, cols].astype(F32) + mm(q_ref[:, cols], s_ref[cols, :])
         parts.append((scaling * total).astype(BF16))
     put_rows(m_ref, jnp.concatenate(parts, axis=1), o_ref)
 
@@ -265,9 +265,9 @@
         cols = slice(h * head, (h + 1) * head)
         q, ag = q_ref[:, cols], ag_ref[:, cols]
         back = jnp.where(t >= s, mm(v_ref[:, cols], ag, NT), 0.0).astype(BF16)
-        gk_ref[:, cols] = scaling * mm(back, q)
+        gk_ref[:, cols] = (scaling * mm(back, q)).astype(BF16)
         scores = jnp.where(t >= s, mm(mk_ref[:, cols], q, NT), 0.0).astype(BF16)
-        gv_ref[:, cols] = scaling * mm(scores, ag)
+        gv_ref[:, cols] = (scaling * mm(scores, ag)).astype(BF16)
 
 
 def final_body(head, mk_ref, v_ref, s_ref, g_ref, gki_ref, gvi_ref, gk_ref, gv_ref):
@@ -276,9 +276,9 @@
     for h in range(width // head):
         cols = slice(h * head, (h + 1) * head)
         state = g_ref[cols, :]
-        gk = gki_ref[:, cols] + mm(v_ref[:, cols], state, NT)
+        gk = gki_ref[:, cols].astype(F32) + mm(v_ref[:, cols], state, NT)
         gk_ref[:, cols] = (gate[:, cols] * gk).astype(BF16)
-        gv_ref[:, cols] = (gvi_ref[:, cols] + mm(mk_ref[:, cols], state)).astype(BF16)
+        gv_ref[:, cols] = (gvi_ref[:, cols].astype(F32) + mm(mk_ref[:, cols], state)).astype(BF16)
 
 
 def shape(*dims, dtype=BF16):
@@ -325,7 +325,6 @@
     tall = pl.BlockSpec((pair, head), lambda i: (i, 0))
     wide = cols(length, pair)
     seq = shape(length, width)
-    seq32 = shape(length, width, dtype=F32)
     unit = length * width * 2
     spikes_t = spikes.T
 
@@ -359,8 +358,8 @@
         pieces[i] = lax.ppermute(pieces[i], "exp", [(j, (j + i) % exp) for j in range(exp)])
     states_in, _ = exchange(block_state, False, ())
     intra = call(
-        functools.partial(intra_body, head), (pairs,), [wide] * 3, wide, seq32,
-        4 * length * length * width, 5 * unit,
+        functools.partial(intra_body, head), (pairs,), [wide] * 3, wide, seq,
+        4 * length * length * width, 4 * unit,
     )(queries, masked, value_vectors)
 
     send_shape = shape(2, 2, half_rows, 2 * width)
@@ -446,7 +445,7 @@
     )(select_t, returned, grad_cols, queries)
     parts = call(
         functools.partial(back_body, head, scaling), (pairs,), [wide] * 4, [wide] * 2,
-        [seq32, seq32], 8 * length * length * width, 8 * unit,
+        [seq, seq], 8 * length * length * width, 6 * unit,
     )(queries, masked, value_vectors, att_grad)
     grad_states, (keys_part, values_part) = exchange(local_grad, True, tuple(parts))
     grad_queries = call(
@@ -456,7 +455,7 @@
     grad_keys, grad_values = call(
         functools.partial(final_body, head), (pairs,),
         [wide, wide, whole(heads, length), tall, wide, wide], [wide] * 2, [seq, seq],
-        4 * length * width * head, 8 * unit, 52,
+        4 * length * width * head, 6 * unit, 52,
     )(masked, value_vectors, spikes_t, grad_states, keys_part, values_part)
     return grad_queries, grad_keys, grad_values, grad_gate[None], grad_up[None], grad_down[None]
 

time: 349 us -> 348 us (level)
  no operation moved by 1% of the time
where the time goes in v5:
time: 348 us; the launch traced here: 347 us
  blocking collectives  154 us (44%)
  Pallas kernels  84.4 us (24%)
  waiting for transfers between devices  65.4 us (19%)
  starting transfers between devices  42.4 us (12%)
    all_to_all x1, blocking collectives, on_device(): lax.all_to_all(buffer.reshape(devices, slots, 2 * width), everywhere, 0,...  154 us
    all_to_all x1, waiting for transfers between devices, on_device(): lax.all_to_all(back_rows.reshape(devices, slots, width), everywhere, 0, 0...  58 us
    all_to_all x4, starting transfers between devices, exchange(): pieces = lax.all_to_all(pieces, 'ctx', 0, 0, tiled=True)  29.2 us
    pallas_call x1, Pallas kernels, on_device(): call(functools.partial(expert_body, exp), (2 * exp,), [pl.BlockSpec((half...  20.3 us
    pallas_call x1, Pallas kernels, on_device(): call(weights_body, (exp,), [pl.BlockSpec((half_rows, width), lambda i: (i...  14.7 us
    all_to_all x1, starting transfers between devices, on_device(): lax.all_to_all(back_rows.reshape(devices, slots, width), everywhere, 0, 0...  8.37 us
    all_to_all x4, waiting for transfers between devices, exchange(): pieces = lax.all_to_all(pieces, 'ctx', 0, 0, tiled=True)  7.41 us
    pallas_call x1, Pallas kernels, on_device(): call(functools.partial(back_body, head, scaling), (pairs,), [wide] * 4, [...  7.32 us
  transfers between devices with their start and end apart: 8, of which 4 were waited for; matrix products, arithmetic and copies ran while one was open for 0% of the time, Pallas kernels for 13%

profile of v5, /device:TPU:1, one launch (start us, length us, event | category | flops | bytes accessed | tf_op | source)
XLA Modules:
  0.0 347.5 jit_solution(6894964779752749961)
XLA Ops:
  0.6 3.2 shard_map.145
  3.8 9.6 %all-to-all-start = ((bf16[32,32,128]{2,1,0:T(8,128)(2,1)}), bf16[32,32,128]{2,1,0:T(8,128)(2,1)S(1)}, u32[]{:S(2)}, u32[]{:S(2)}) async-start(bf16[32,32,128]{2,1,0:T(8,128)(2,1)} %bitcast.29), calls=%async_computation | async-start | bytes 524288 | tf_op jit(solution)/shard_map/all_to_all | solution.py:333
  13.4 2.4 shard_map.146
  15.8 1.2 collective-permute-start
  17.0 2.5 collective-permute-start.1
  19.5 1.2 collective-permute-start.2
  20.6 1.8 all-to-all-done.x_ref
  22.4 0.8 shard_map.149
  23.2 6.4 %all-to-all-start.1 = ((bf16[32,32,128]{2,1,0:T(8,128)(2,1)}), bf16[32,32,128]{2,1,0:T(8,128)(2,1)S(1)}, u32[]{:S(2)}, u32[]{:S(2)}) async-start(bf16[32,32,128]{2,1,0:T(8,128)(2,1)} %shard_map.149), calls=%async_computation.1 | async-start | bytes 524288 | tf_op jit(solution)/shard_map/all_to_all | solution.py:339
  29.6 4.9 %shard_map.148.intra_ref = bf16[512,1024]{1,0:T(8,128)(2,1)} custom-call(bf16[512,1024]{1,0:T(8,128)(2,1)} %q_ref.7, bf16[512,1024]{1,0:T(8,128)(2,1)} %get-tuple-element.41.mk_ref, bf16[512,1024]{1,0:T(8,128)(2,1)} %v_ref.9), custom_call_target="tpu_custom_call" | custom-call | flops 1073741824 | bytes 4194304 | tf_op jit(solution)/shard_map/pallas_call | solution.py:360
  34.5 0.0 copy-start
  34.5 0.0 collective-permute-done.refs_1_
  34.5 0.0 copy-start.4
  34.5 0.0 collective-permute-done.1.refs_2_
  34.5 0.0 copy-start.5
  34.6 0.0 collective-permute-done.2.refs_3_
  34.6 0.0 copy-start.6
  34.6 0.7 copy-done.4
  35.2 0.1 copy-done.5
  35.3 0.1 copy-done.6
  35.4 6.7 %shard_map.147 = (bf16[512,1024]{1,0:T(8,128)(2,1)}, bf16[1536,512]{1,0:T(8,128)(2,1)}, bf16[2,2,768,2048]{3,2,1,0:T(8,128)(2,1)}) custom-call(s32[1]{0:T(128)} %bitcast.1.mine_ref, bf16[144,1024]{1,0:T(8,128)(2,1)} %get-tuple-element.53.refs_0_, bf16[144,1024]{1,0:T(8,128)(2,1)} %copy-done.4, bf16[144,1024]{1,0:T(8,128)(2,1)} %copy-done.5, ...), custom_call_target="tpu_custom_call" | custom-call | flops 1610612736 | bytes 9961472 | tf_op jit(solution)/shard_map/pallas_call | solution.py:368
  42.1 0.0 all-to-all-done.1
  42.1 0.0 copy-start.2
  42.1 0.0 copy-done
  42.1 5.9 %shard_map.150 = bf16[2,2,768,2048]{3,2,1,0:T(8,128)(2,1)} custom-call(bf16[1536,512]{1,0:T(8,128)(2,1)} %get-tuple-element.48.m_ref, bf16[512,1024]{1,0:T(8,128)(2,1)S(1)} %copy-done, bf16[512,1024]{1,0:T(8,128)(2,1)} %shard_map.148.intra_ref, bf16[1024,128]{1,0:T(8,128)(2,1)S(1)} %bitcast.18, ...), custom_call_target="tpu_custom_call", output_to_operand_aliasing={{}: (4, {})} | custom-call | flops 1610612736 | bytes 9961472 | tf_op jit(solution)/shard_map/pallas_call | solution.py:377
  48.0 0.0 copy-done.2
  48.0 153.7 %all_to_all.30 = bf16[128,24,2048]{2,1,0:T(8,128)(2,1)} all-to-all(bf16[128,24,2048]{2,1,0:T(8,128)(2,1)} %bitcast.27), channel_id=1, replica_groups=mesh['ctx'=32,'exp'=4] {'exp','ctx'}, dimensions={0} | all-to-all | bytes 25165824 | tf_op jit(solution)/shard_map/all_to_all | solution.py:383
  201.6 20.3 %shard_map.151 = (bf16[3072,1024]{1,0:T(8,128)(2,1)}, bf16[768,384]{1,0:T(8,128)(2,1)}, bf16[768,768]{1,0:T(8,128)(2,1)}) custom-call(bf16[3072,2048]{1,0:T(8,128)(2,1)} %bitcast.23, bf16[3072,2048]{1,0:T(8,128)(2,1)} %bitcast.24, bf16[4096,384]{1,0:T(8,128)(2,1)} %bitcast.33, bf16[4096,384]{1,0:T(8,128)(2,1)} %bitcast.34, bf16[384,4096]{1,0:T(8,128)(2,1)} %bitcast.35), custom_call_target="tpu_custom_call" | custom-call | flops 12079595520 | bytes 34603008 | tf_op jit(solution)/shard_map/pallas_call | solution.py:390
  221.9 8.4 %all-to-all-start.3 = ((bf16[128,24,1024]{2,1,0:T(8,128)(2,1)}), bf16[128,24,1024]{2,1,0:T(8,128)(2,1)}, u32[]{:S(2)}, u32[]{:S(2)}) async-start(bf16[128,24,1024]{2,1,0:T(8,128)(2,1)} %bitcast.28), calls=%async_computation.3 | async-start | bytes 12582912 | tf_op jit(solution)/shard_map/all_to_all | solution.py:411
  230.3 2.9 shard_map.152.mt_ref
  233.2 14.7 %shard_map.153 = (bf16[4096,384]{1,0:T(8,128)(2,1)}, bf16[4096,384]{1,0:T(8,128)(2,1)}, bf16[384,4096]{1,0:T(8,128)(2,1)}) custom-call(bf16[3072,2048]{1,0:T(8,128)(2,1)} %bitcast.25, bf16[3072,2048]{1,0:T(8,128)(2,1)} %bitcast.26, bf16[768,384]{1,0:T(8,128)(2,1)} %get-tuple-element.57.h_ref, bf16[768,768]{1,0:T(8,128)(2,1)} %get-tuple-element.52.a_ref), custom_call_target="tpu_custom_call" | custom-call | flops 7247757312 | bytes 22020096 | tf_op jit(solution)/shard_map/pallas_call | solution.py:414
  247.9 58.0 %all-to-all-done.3 = bf16[128,24,1024]{2,1,0:T(8,128)(2,1)} async-done(((bf16[128,24,1024]{2,1,0:T(8,128)(2,1)}), bf16[128,24,1024]{2,1,0:T(8,128)(2,1)}, u32[]{:S(2)}, u32[]{:S(2)}) %all-to-all-start.3) | async-done | bytes 6291488 | tf_op jit(solution)/shard_map/all_to_all | solution.py:411
  305.9 6.1 %shard_map.154 = (bf16[512,1024]{1,0:T(8,128)(2,1)}, bf16[1024,128]{1,0:T(8,128)(2,1)}) custom-call(bf16[512,1536]{1,0:T(8,128)(2,1)} %shard_map.152.mt_ref, bf16[4,768,1024]{2,1,0:T(8,128)(2,1)} %bitcast.12.ret_ref, bf16[512,1024]{1,0:T(8,128)(2,1)} %get-tuple-element.63.og_ref, bf16[512,1024]{1,0:T(8,128)(2,1)} %q_ref.7), custom_call_target="tpu_custom_call" | custom-call | flops 1610612736 | bytes 11010048 | tf_op jit(solution)/shard_map/pallas_call | solution.py:440
  311.9 7.5 %all-to-all-start.4 = ((bf16[32,32,128]{2,1,0:T(8,128)(2,1)}), bf16[32,32,128]{2,1,0:T(8,128)(2,1)S(1)}, u32[]{:S(2)}, u32[]{:S(2)}) async-start(bf16[32,32,128]{2,1,0:T(8,128)(2,1)} %bitcast.30), calls=%async_computation.4 | async-start | bytes 524288 | tf_op jit(solution)/shard_map/all_to_all | solution.py:333
  319.4 7.3 %shard_map.156 = (bf16[512,1024]{1,0:T(8,128)(2,1)}, bf16[512,1024]{1,0:T(8,128)(2,1)}) custom-call(bf16[512,1024]{1,0:T(8,128)(2,1)} %q_ref.7, bf16[512,1024]{1,0:T(8,128)(2,1)} %get-tuple-element.41.mk_ref, bf16[512,1024]{1,0:T(8,128)(2,1)} %v_ref.9, bf16[512,1024]{1,0:T(8,128)(2,1)} %get-tuple-element.64.ag_ref), custom_call_target="tpu_custom_call" | custom-call | flops 2147483648 | bytes 6291456 | tf_op jit(solution)/shard_map/pallas_call | solution.py:446
  326.7 0.0 copy-start.1
  326.7 0.0 copy-start.3
  326.7 1.6 all-to-all-done.4.x_ref
  328.4 0.7 shard_map.157
  329.1 5.7 %all-to-all-start.5 = ((bf16[32,32,128]{2,1,0:T(8,128)(2,1)}), bf16[32,32,128]{2,1,0:T(8,128)(2,1)S(1)}, u32[]{:S(2)}, u32[]{:S(2)}) async-start(bf16[32,32,128]{2,1,0:T(8,128)(2,1)} %shard_map.157), calls=%async_computation.5 | async-start | bytes 524288 | tf_op jit(solution)/shard_map/all_to_all | solution.py:339
  334.9 5.0 %shard_map.155 = bf16[512,1024]{1,0:T(8,128)(2,1)} custom-call(bf16[512,1024]{1,0:T(8,128)(2,1)} %get-tuple-element.41.mk_ref, bf16[512,1024]{1,0:T(8,128)(2,1)} %v_ref.9, bf16[512,1024]{1,0:T(8,128)(2,1)} %get-tuple-element.64.ag_ref, bf16[1024,128]{1,0:T(8,128)(2,1)} %bitcast.19), custom_call_target="tpu_custom_call" | custom-call | flops 1073741824 | bytes 4194304 | tf_op jit(solution)/shard_map/pallas_call | solution.py:451
  339.9 4.0 %all-to-all-done.5 = bf16[32,32,128]{2,1,0:T(8,128)(2,1)S(1)} async-done(((bf16[32,32,128]{2,1,0:T(8,128)(2,1)}), bf16[32,32,128]{2,1,0:T(8,128)(2,1)S(1)}, u32[]{:S(2)}, u32[]{:S(2)}) %all-to-all-start.5) | async-done | bytes 262176 | tf_op jit(solution)/shard_map/all_to_all | solution.py:339
  343.9 0.0 copy-done.1
  343.9 0.0 copy-done.3
  343.9 3.6 %shard_map.158 = (bf16[512,1024]{1,0:T(8,128)(2,1)}, bf16[512,1024]{1,0:T(8,128)(2,1)}) custom-call(bf16[512,1024]{1,0:T(8,128)(2,1)S(1)} %copy-done.1, bf16[512,1024]{1,0:T(8,128)(2,1)} %v_ref.9, s32[8,512]{1,0:T(8,128)S(1)} %bitcast.22, bf16[1024,128]{1,0:T(8,128)(2,1)S(1)} %bitcast.20, bf16[512,1024]{1,0:T(8,128)(2,1)} %get-tuple-element.69.gki_ref, ...), custom_call_target="tpu_custom_call" | custom-call | flops 268435456 | bytes 6291456 | tf_op jit(solution)/shard_map/pallas_call | solution.py:455
Async XLA Ops:
  3.8 18.6 %all-to-all-start = ((bf16[32,32,128]{2,1,0:T(8,128)(2,1)}), bf16[32,32,128]{2,1,0:T(8,128)(2,1)S(1)}, u32[]{:S(2)}, u32[]{:S(2)}) async-start(bf16[32,32,128]{2,1,0:T(8,128)(2,1)} %bitcast.29), calls=%async_computation | async-start | bytes 524288 | tf_op jit(solution)/shard_map/all_to_all | solution.py:333
  15.8 18.7 %collective-permute-start = (bf16[144,1024]{1,0:T(8,128)(2,1)}, bf16[144,1024]{1,0:T(8,128)(2,1)S(1)}, u32[]{:S(2)}, u32[]{:S(2)}) collective-permute-start(bf16[144,1024]{1,0:T(8,128)(2,1)} %get-tuple-element.45), channel_id=1, source_target_pairs={{0,1},{1,2},{2,3},{3,0},{4,5},{5,6},{6,7},{7,4},{8,9},{9,10},{10,1... | collective-permute-start | bytes 884744 | tf_op jit(solution)/shard_map/ppermute | solution.py:358
  17.0 17.5 %collective-permute-start.1 = (bf16[144,1024]{1,0:T(8,128)(2,1)}, bf16[144,1024]{1,0:T(8,128)(2,1)S(1)}, u32[]{:S(2)}, u32[]{:S(2)}) collective-permute-start(bf16[144,1024]{1,0:T(8,128)(2,1)} %get-tuple-element.46), channel_id=1, source_target_pairs={{0,2},{1,3},{2,0},{3,1},{4,6},{5,7},{6,4},{7,5},{8,10},{9,11},{10,... | collective-permute-start | bytes 884744 | tf_op jit(solution)/shard_map/ppermute | solution.py:358
  19.5 15.1 %collective-permute-start.2 = (bf16[144,1024]{1,0:T(8,128)(2,1)}, bf16[144,1024]{1,0:T(8,128)(2,1)S(1)}, u32[]{:S(2)}, u32[]{:S(2)}) collective-permute-start(bf16[144,1024]{1,0:T(8,128)(2,1)} %get-tuple-element.47), channel_id=1, source_target_pairs={{0,3},{1,0},{2,1},{3,2},{4,7},{5,4},{6,5},{7,6},{8,11},{9,8},{10,9... | collective-permute-start | bytes 884744 | tf_op jit(solution)/shard_map/ppermute | solution.py:358
  23.2 18.9 %all-to-all-start.1 = ((bf16[32,32,128]{2,1,0:T(8,128)(2,1)}), bf16[32,32,128]{2,1,0:T(8,128)(2,1)S(1)}, u32[]{:S(2)}, u32[]{:S(2)}) async-start(bf16[32,32,128]{2,1,0:T(8,128)(2,1)} %shard_map.149), calls=%async_computation.1 | async-start | bytes 524288 | tf_op jit(solution)/shard_map/all_to_all | solution.py:339
  34.5 7.6 %copy-start = (bf16[512,1024]{1,0:T(8,128)(2,1)S(1)}, bf16[512,1024]{1,0:T(8,128)(2,1)}, u32[]{:S(2)}) copy-start(bf16[512,1024]{1,0:T(8,128)(2,1)} %q_ref.7) | copy-start | bytes 3145732
  34.5 0.7 copy-start.4
  34.5 0.8 copy-start.5
  34.6 0.9 copy-start.6
  42.1 5.9 %copy-start.2 = (bf16[32,32,128]{2,1,0:T(8,128)(2,1)}, bf16[32,32,128]{2,1,0:T(8,128)(2,1)S(1)}, u32[]{:S(2)}) copy-start(bf16[32,32,128]{2,1,0:T(8,128)(2,1)S(1)} %all-to-all-done.1) | copy-start | bytes 786436
  221.9 83.9 %all-to-all-start.3 = ((bf16[128,24,1024]{2,1,0:T(8,128)(2,1)}), bf16[128,24,1024]{2,1,0:T(8,128)(2,1)}, u32[]{:S(2)}, u32[]{:S(2)}) async-start(bf16[128,24,1024]{2,1,0:T(8,128)(2,1)} %bitcast.28), calls=%async_computation.3 | async-start | bytes 12582912 | tf_op jit(solution)/shard_map/all_to_all | solution.py:411
  311.9 16.4 %all-to-all-start.4 = ((bf16[32,32,128]{2,1,0:T(8,128)(2,1)}), bf16[32,32,128]{2,1,0:T(8,128)(2,1)S(1)}, u32[]{:S(2)}, u32[]{:S(2)}) async-start(bf16[32,32,128]{2,1,0:T(8,128)(2,1)} %bitcast.30), calls=%async_computation.4 | async-start | bytes 524288 | tf_op jit(solution)/shard_map/all_to_all | solution.py:333
  326.7 17.1 %copy-start.1 = (bf16[512,1024]{1,0:T(8,128)(2,1)S(1)}, bf16[512,1024]{1,0:T(8,128)(2,1)}, u32[]{:S(2)}) copy-start(bf16[512,1024]{1,0:T(8,128)(2,1)} %get-tuple-element.41.mk_ref) | copy-start | bytes 3145732
  326.7 17.1 %copy-start.3 = (s32[512,8]{0,1:T(8,128)S(1)}, s32[512,8]{0,1:T(8,128)}, u32[]{:S(2)}) copy-start(s32[512,8]{0,1:T(8,128)} %param.13) | copy-start | bytes 49156
  329.1 14.7 %all-to-all-start.5 = ((bf16[32,32,128]{2,1,0:T(8,128)(2,1)}), bf16[32,32,128]{2,1,0:T(8,128)(2,1)S(1)}, u32[]{:S(2)}, u32[]{:S(2)}) async-start(bf16[32,32,128]{2,1,0:T(8,128)(2,1)} %shard_map.157), calls=%async_computation.5 | async-start | bytes 524288 | tf_op jit(solution)/shard_map/all_to_all | solution.py:339
